TPU v7x, 32 devices: a whole 2x2x4 slice. The times are simulated.
32 devices in a mesh: pts: 16 (over z, x, core), modes: 2 (over y).
Axes of the slice: x: 2, y: 2, z: 4, core: 2. Of those that a mesh axis runs over, the one named last changes fastest.
Arguments:
- features: bfloat16 [65536, 128], P('pts'), may hold values from -6 to 6
- coords: float32 [3, 65536], P(None, 'pts'), may hold values from 0 to 1
- quad_weight: float32 [65536], P('pts'), may hold values from 0.5 to 6, as said below
- mode_table: int32 [3, 8192], replicated, may hold values from -8 to 31, as said below
- mode_weight: bfloat16 [8192, 2, 128, 128], P(('pts', 'modes')), may hold values from -4 to 4
- lin_weight: bfloat16 [128, 128], replicated, may hold values from -0.5 to 0.5
- bias: float32 [128], replicated, may hold values from -3 to 3
Outputs:
- output: bfloat16 [65536, 128], P(('pts', 'modes'))
Inputs may be any that keep to these rules, and one draw needn't show every extreme that they name: `mode_table`: each column is a distinct triple (kx, ky, kz) with -8 <= kx < 8, -8 <= ky < 8, 0 <= kz < 32; every such triple appears exactly once, in an order drawn from the seed. `quad_weight`: Positive.
All inputs are finite; a program needn't handle non-finite values.
Results may differ from a plain program's by a relative error of at most 0.018.
Values may be sent and summed in bfloat16 or wider, within the bound.
A program may use at most 128 MiB of HBM per device.

v0:
```python
import math

import jax
import jax.numpy as jnp
from jax import lax
from jax.sharding import PartitionSpec as P


def phase_basis(coords, wave):
    turns = coords[0][:, None] * wave[0][None, :] + coords[1][:, None] * wave[1][None, :]
    turns = turns + coords[2][:, None] * wave[2][None, :]
    angle = 2.0 * math.pi * turns
    return jnp.concatenate([jnp.cos(angle), -jnp.sin(angle)], axis=1).astype(jnp.bfloat16)


def on_device(features, coords, quad_weight, mode_table, mode_weight, lin_weight, bias):
    width = features.shape[1]
    local_pts = features.shape[0]
    own_modes = mode_weight.shape[0]
    n_pts = lax.axis_size("pts")
    n_groups = lax.axis_size("modes")
    group = lax.axis_index("modes")
    group_modes = n_pts * own_modes
    weighted = (quad_weight[:, None] * features.astype(jnp.float32)).astype(jnp.bfloat16)
    total = lax.psum(jnp.sum(quad_weight), "pts")
    wave_all = mode_table.astype(jnp.float32)
    grouped = wave_all.reshape(3, n_pts, n_groups, own_modes)
    wave_group = lax.dynamic_slice_in_dim(grouped, group, 1, 2).reshape(3, group_modes)
    basis_all = phase_basis(coords, wave_group)

    def pick_columns(rows):
        cosine = lax.slice_in_dim(basis_all, 0, rows, axis=1)
        sine = lax.dynamic_slice_in_dim(basis_all, group_modes, rows, 1)
        return jnp.concatenate([cosine, sine], axis=1)

    basis = pick_columns(lax.axis_size("pts") * own_modes)
    term = lax.dot_general(
        basis, weighted, (((0,), (0,)), ((), ())), preferred_element_type=jnp.float32
    )
    coef = lax.psum_scatter(
        term.reshape(2, lax.axis_size("pts") * own_modes, width)
        .transpose(1, 0, 2)
        .reshape(lax.axis_size("pts") * own_modes, 2 * width)
        .astype(jnp.bfloat16),
        "pts",
        scatter_dimension=0,
        tiled=True,
    )
    real_in = coef[:, :width]
    imag_in = coef[:, width:]
    w_real = mode_weight[:, 0]
    w_imag = mode_weight[:, 1]
    real_out = jnp.einsum(
        "mc,mcd->md", real_in, w_real, preferred_element_type=jnp.float32
    ) - jnp.einsum("mc,mcd->md", imag_in, w_imag, preferred_element_type=jnp.float32)
    imag_out = jnp.einsum(
        "mc,mcd->md", real_in, w_imag, preferred_element_type=jnp.float32
    ) + jnp.einsum("mc,mcd->md", imag_in, w_real, preferred_element_type=jnp.float32)
    filtered = jnp.concatenate([real_out, imag_out], axis=1).astype(jnp.bfloat16)
    out_rows = local_pts // n_groups
    my_features = lax.dynamic_slice_in_dim(features, group * out_rows, out_rows, 0)
    piece = lax.all_gather(filtered, "pts", axis=0, tiled=True)
    basis = pick_columns(piece.shape[0])
    rhs = jnp.concatenate([piece[:, :width], piece[:, width:]], axis=0)
    field = jnp.dot(basis, rhs, preferred_element_type=jnp.float32)
    spectral = lax.psum_scatter(
        field.astype(jnp.bfloat16), "modes", scatter_dimension=0, tiled=True
    ).astype(jnp.float32)
    linear = jnp.dot(my_features, lin_weight, preferred_element_type=jnp.float32)
    pre = spectral / total + linear + bias[None, :]
    return jax.nn.gelu(pre, approximate=False).astype(jnp.bfloat16)


def solution(mesh):
    return jax.shard_map(
        on_device,
        mesh=mesh,
        in_specs=(
            P("pts", None),
            P(None, "pts"),
            P("pts"),
            P(),
            P(("pts", "modes"), None, None, None),
            P(),
            P(),
        ),
        out_specs=P(("pts", "modes"), None),
        check_vma=False,
    )
```

profile of v0, /device:TPU:0, one launch (start us, length us, event | category | flops | bytes accessed | tf_op | source)
XLA Modules:
  0.0 505.3 jit_solution(14802626488108388729)
XLA Ops:
  6.5 0.0 copy-start
  6.5 0.0 reduce-scatter.3.cloned.1.call-start
  6.5 0.9 convert_element_type.32
  7.5 0.1 reshape.19
  7.6 1.0 fusion.36
  8.6 0.1 constant_dynamic-slice_fusion.1
  8.7 0.0 copy-start.1
  8.7 0.0 copy-start.2
  8.7 264.3 %cosine_convert_fusion = (bf16[4096,4096]{1,0:T(8,128)(2,1)}, bf16[4096,4096]{1,0:T(8,128)(2,1)}) fusion(f32[4096]{0:T(1024)S(1)} %bitcast.45, f32[4096]{0:T(1024)S(1)} %bitcast.47, f32[4096]{0:T(1024)S(1)} %bitcast.44, f32[4096]{0:T(1024)S(1)} %bitcast.48, f32[4096]{0:T(1024)S(1)} %bitcast.43, f32[4096]{0:T(1024)S(1)} %bitcast.46), kind=kLoop, calls=%fused_computation.2 | loop fusion | flops 150994944 | bytes 67207168 | tf_op jit(solution)/shard_map/convert.2
  273.0 0.0 copy-done.1
  273.0 0.0 copy-done.2
  273.0 27.4 %fusion.2 = bf16[8192,128]{1,0:T(8,128)(2,1)S(1)} fusion(bf16[4096,4096]{1,0:T(8,128)(2,1)} %get-tuple-element.10, bf16[4096,4096]{1,0:T(8,128)(2,1)} %get-tuple-element.9, bf16[4096,128]{1,0:T(8,128)(2,1)S(1)} %copy-done.2, f32[4096]{0:T(1024)S(1)} %copy-done.1), kind=kOutput, calls=%fused_computation.6 | convolution fusion | flops 8726773760 | bytes 70270976 | tf_op jit(solution)/shard_map/dot_general | solution.py:37
  300.3 2.8 copy.8
  303.1 0.0 reduce-scatter.3.cloned.1.call-update
  303.2 0.2 all-gather.2.cloned.1.call-start
  303.4 64.5 %reduce-scatter.3.cloned.1.call-done = bf16[256,256]{0,1:T(8,128)(2,1)} async-done(((bf16[4096,256]{0,1:T(8,128)(2,1)}), bf16[256,256]{0,1:T(8,128)(2,1)}) %reduce-scatter.3.cloned.1.call-update) | async-done | bytes 131088 | tf_op jit(solution)/shard_map/reduce_scatter | solution.py:40
  367.9 0.9 slice_bitcast_fusion
  368.8 0.1 copy.9
  368.9 5.7 %fusion.9 = f32[256,1,128]{2,1,0:T(1,128)S(1)} fusion(bf16[256,128,1]{1,2,0:T(2,128)(2,1)S(1)} %copy.9, bf16[256,2,128,128]{3,2,1,0:T(8,128)(2,1)} %param.11), kind=kOutput, calls=%fused_computation.13 | convolution fusion | flops 8388608 | bytes 8585216 | tf_op jit(solution)/shard_map/mc,mcd->md/dot_general | solution.py:53
  374.6 5.7 %fusion.3 = f32[256,1,128]{2,1,0:T(1,128)S(1)} fusion(bf16[256,128,1]{1,2,0:T(2,128)(2,1)S(1)} %copy.9, bf16[256,2,128,128]{3,2,1,0:T(8,128)(2,1)} %param.11), kind=kOutput, calls=%fused_computation.7 | convolution fusion | flops 8388608 | bytes 8585216 | tf_op jit(solution)/shard_map/mc,mcd->md/dot_general | solution.py:56
  380.3 0.1 copy.11
  380.4 5.7 %fusion.5 = f32[256,1,128]{2,1,0:T(1,128)S(1)} fusion(bf16[256,128,1]{1,2,0:T(2,128)(2,1)S(1)} %copy.11, bf16[256,2,128,128]{3,2,1,0:T(8,128)(2,1)} %param.11), kind=kOutput, calls=%fused_computation.9 | convolution fusion | flops 8388608 | bytes 8585216 | tf_op jit(solution)/shard_map/mc,mcd->md/dot_general | solution.py:55
  386.1 5.7 %fusion.7 = f32[256,1,128]{2,1,0:T(1,128)S(1)} fusion(bf16[256,128,1]{1,2,0:T(2,128)(2,1)S(1)} %copy.11, bf16[256,2,128,128]{3,2,1,0:T(8,128)(2,1)} %param.11), kind=kOutput, calls=%fused_computation.11 | convolution fusion | flops 8388608 | bytes 8585216 | tf_op jit(solution)/shard_map/mc,mcd->md/dot_general | solution.py:58
  391.9 0.7 pad_maximum_fusion.7
  392.5 0.0 all-gather.2.cloned.1.call-update
  392.6 0.0 reduce-scatter.5.cloned.1.call-start
  392.6 40.5 %all-gather.2.cloned.1.call-done = bf16[4096,256]{1,0:T(8,128)(2,1)} async-done(((bf16[256,256]{1,0:T(8,128)(2,1)}), bf16[4096,256]{1,0:T(8,128)(2,1)}) %all-gather.2.cloned.1.call-update) | async-done | bytes 2097168 | tf_op jit(solution)/shard_map/all_gather | solution.py:62
  433.1 1.7 fusion.35
  434.8 0.0 copy-start.3
  434.8 26.5 %fusion.15 = bf16[4096,128]{1,0:T(8,128)(2,1)} fusion(bf16[4096,4096]{1,0:T(8,128)(2,1)} %get-tuple-element.10, bf16[4096,4096]{1,0:T(8,128)(2,1)} %get-tuple-element.9, bf16[4096,128]{1,0:T(8,128)(2,1)S(1)} %get-tuple-element.6, bf16[4096,128]{1,0:T(8,128)(2,1)S(1)} %get-tuple-element.5), kind=kOutput, calls=%fused_computation.19 | convolution fusion | flops 8728870912 | bytes 70254592 | tf_op jit(solution)/shard_map/dot_general | solution.py:65
  461.3 0.0 reduce-scatter.5.cloned.1.call-update
  461.3 0.6 reduce_sum.9
  461.9 32.0 %psum.7 = f32[]{:T(128)} all-reduce(f32[]{:T(128)} %reduce_sum.9), channel_id=1, replica_groups=mesh['pts'=16,'modes'=2] {'pts'}, use_global_device_ids=true, to_apply=%region_3.0 | all-reduce | flops 1 | bytes 8 | tf_op jit(solution)/shard_map/psum | solution.py:25
  493.9 0.0 reduce-scatter.5.cloned.1.call-done
  493.9 0.0 copy-done
  493.9 0.0 copy-done.3
  493.9 4.9 fusion.22
  (1 shorter events, 0.0 us)
Async XLA Ops:
  6.5 487.3 %copy-start = (bf16[128,128]{1,0:T(8,128)(2,1)S(1)}, bf16[128,128]{1,0:T(8,128)(2,1)}, u32[]{:S(2)}) copy-start(bf16[128,128]{1,0:T(8,128)(2,1)} %param.12) | copy-start | bytes 98308
  6.5 361.4 %reduce-scatter.3.cloned.1.call-start = ((), (), s32[]{:S(2)}) async-start(), calls=%async_computation.2 | async-start | bytes 2228224 | tf_op jit(solution)/shard_map/reduce_scatter | solution.py:40
  8.7 264.3 %copy-start.1 = (f32[4096]{0:T(1024)S(1)}, f32[4096]{0:T(1024)}, u32[]{:S(2)}) copy-start(f32[4096]{0:T(1024)} %param.9) | copy-start | bytes 49156
  8.7 264.3 %copy-start.2 = (bf16[4096,128]{1,0:T(8,128)(2,1)S(1)}, bf16[4096,128]{1,0:T(8,128)(2,1)}, u32[]{:S(2)}) copy-start(bf16[4096,128]{1,0:T(8,128)(2,1)} %param.7) | copy-start | bytes 3145732
  303.2 129.9 %all-gather.2.cloned.1.call-start = ((), (), s32[]{:S(2)}) async-start(), calls=%async_computation.3 | async-start | bytes 2228224 | tf_op jit(solution)/shard_map/all_gather | solution.py:62
  392.6 101.3 %reduce-scatter.5.cloned.1.call-start = ((), (), s32[]{:S(2)}) async-start(), calls=%async_computation.4 | async-start | bytes 1572864 | tf_op jit(solution)/shard_map/reduce_scatter | solution.py:66
  434.8 59.1 %copy-start.3 = (f32[128]{0:T(128)S(1)}, f32[128]{0:T(128)}, u32[]{:S(2)}) copy-start(f32[128]{0:T(128)} %param.13) | copy-start | bytes 1540
Sparse Core Ops, SparseCore 0:
  303.3 64.5 reduce-scatter.2
  392.7 40.3 all-gather.1
  461.4 19.1 reduce-scatter.4
where the time goes:
time: 506 us; the launch traced here: 505 us
  other arithmetic  267 us (53%)
  waiting for transfers between devices  105 us (21%)
  matrix products  81.5 us (16%)
  blocking collectives  32 us (6%)
  between operations  13.2 us (3%)
  local copies, waits for them, and re-layouts  6.8 us (1%)
    another operation x2, other arithmetic  264 us
    reduce_scatter x1, waiting for transfers between devices, on_device(): lax.psum_scatter(term.reshape(2, lax.axis_size('pts') * own_modes, width)...  64.5 us
    all_gather x1, waiting for transfers between devices, on_device(): piece = lax.all_gather(filtered, 'pts', axis=0, tiled=True)  40.5 us
    psum x1, blocking collectives, on_device(): total = lax.psum(jnp.sum(quad_weight), 'pts')  32 us
    dot_general x1, matrix products, on_device(): lax.dot_general(basis, weighted, (((0,), (0,)), ((), ())), preferred_elem...  27.4 us
    dot_general x1, matrix products, on_device(): field = jnp.dot(basis, rhs, preferred_element_type=jnp.float32)  26.5 us
  transfers between devices with their start and end apart: 3, of which 2 were waited for; matrix products, arithmetic and copies ran while one was open for 0% of the time, Pallas kernels for 0%

commit v1 on v0

v1 whole, which is shorter than its diff:
```python
import math

import jax
import jax.numpy as jnp
from jax import lax
from jax.sharding import PartitionSpec as P

KX_LOW, KX_COUNT = -8, 16
KY_LOW, KY_COUNT = -8, 16
KZ_LOW, KZ_COUNT = 0, 32
HALF = KX_COUNT // 2
PLANE = KY_COUNT * KZ_COUNT
AXES = ("pts", "modes")


def cos_sin(turns):
    angle = (2.0 * math.pi) * (turns - jnp.round(turns))
    return jnp.cos(angle), jnp.sin(angle)


def factors(coords):
    x, y, z = coords[0], coords[1], coords[2]
    j = jnp.arange(HALF, dtype=jnp.float32) + 0.5
    xc, xs = cos_sin(j[:, None] * x[None, :])
    ky = jnp.arange(KY_COUNT, dtype=jnp.float32) + KY_LOW
    kz = jnp.arange(KZ_COUNT, dtype=jnp.float32) + KZ_LOW
    yc, ys = cos_sin(ky[:, None] * y[None, :])
    zc, zs = cos_sin(kz[:, None] * z[None, :] - 0.5 * x[None, :])
    yc, ys = yc[:, None, :], ys[:, None, :]
    zc, zs = zc[None], zs[None]
    e_re = (yc * zc - ys * zs).reshape(PLANE, -1)
    e_im = (ys * zc + yc * zs).reshape(PLANE, -1)
    e = jnp.concatenate([e_re, e_im], axis=0).astype(jnp.bfloat16)
    return jnp.concatenate([xc, xs], axis=0), e


def grid_index(mode_table):
    kx = mode_table[0]
    slot = jnp.where(kx >= 0, kx, HALF - 1 - kx)
    return (slot * KY_COUNT + mode_table[1] - KY_LOW) * KZ_COUNT + mode_table[2] - KZ_LOW


def inverse_index(index):
    n = index.shape[0]
    lo = 128
    hi = n // lo
    ids = jnp.arange(n, dtype=jnp.int32)
    hot_lo = (index[:, None] % lo == jnp.arange(lo)[None, :]).astype(jnp.bfloat16)
    hit = index[None, :] // lo == jnp.arange(hi)[:, None]
    top = jnp.where(hit, ids[None, :] // lo, 0).astype(jnp.bfloat16)
    low = jnp.where(hit, ids[None, :] % lo, 0).astype(jnp.bfloat16)
    got = jnp.dot(jnp.concatenate([top, low], axis=0), hot_lo, preferred_element_type=jnp.float32)
    return (got[:hi] * lo + got[hi:]).astype(jnp.int32).reshape(n)


def on_device(features, coords, quad_weight, mode_table, mode_weight, lin_weight, bias):
    width = features.shape[1]
    n_groups = lax.axis_size("modes")
    group = lax.axis_index("modes")
    rows = features.shape[0] // n_groups
    total = lax.psum(jnp.sum(quad_weight), "pts")
    features = lax.dynamic_slice_in_dim(features, group * rows, rows, 0)
    coords = lax.dynamic_slice_in_dim(coords, group * rows, rows, 1)
    quad = lax.dynamic_slice_in_dim(quad_weight, group * rows, rows, 0)
    xf, e = factors(coords)
    index = grid_index(mode_table)
    inverse = inverse_index(index)
    weighted = (quad[:, None] * features.astype(jnp.float32)).astype(jnp.bfloat16)
    xw = (xf.T[:, :, None] * weighted.astype(jnp.float32)[:, None, :]).astype(jnp.bfloat16)
    term = jnp.dot(e, xw.reshape(rows, KX_COUNT * width), preferred_element_type=jnp.float32)
    term = term.reshape(2, PLANE, 2, HALF, width)
    a, b, c, d = term[0, :, 0], term[1, :, 1], term[1, :, 0], term[0, :, 1]
    pos = jnp.concatenate([a - b, -(c + d)], axis=-1)
    neg = jnp.concatenate([a + b, d - c], axis=-1)
    coef = jnp.concatenate([pos, neg], axis=1).astype(jnp.bfloat16)
    coef = coef.transpose(1, 0, 2).reshape(KX_COUNT * PLANE, 2 * width)
    coef = jnp.take(coef, index, axis=0, mode="clip")
    coef = lax.psum_scatter(coef, AXES, scatter_dimension=0, tiled=True)
    real_in = coef[:, :width]
    imag_in = coef[:, width:]
    w_real = mode_weight[:, 0]
    w_imag = mode_weight[:, 1]
    real_out = jnp.einsum(
        "mc,mcd->md", real_in, w_real, preferred_element_type=jnp.float32
    ) - jnp.einsum("mc,mcd->md", imag_in, w_imag, preferred_element_type=jnp.float32)
    imag_out = jnp.einsum(
        "mc,mcd->md", real_in, w_imag, preferred_element_type=jnp.float32
    ) + jnp.einsum("mc,mcd->md", imag_in, w_real, preferred_element_type=jnp.float32)
    filtered = jnp.concatenate([real_out, imag_out], axis=1).astype(jnp.bfloat16)
    full = lax.all_gather(filtered, AXES, axis=0, tiled=True)
    full = jnp.take(full, inverse, axis=0, mode="clip").astype(jnp.float32)
    full = full.reshape(2, HALF, PLANE, 2, width)
    pos_re, pos_im = full[0, :, :, 0], full[0, :, :, 1]
    neg_re, neg_im = full[1, :, :, 0], full[1, :, :, 1]
    by_re = jnp.concatenate([pos_re + neg_re, neg_im - pos_im], axis=0)
    by_im = jnp.concatenate([-(pos_im + neg_im), neg_re - pos_re], axis=0)
    rhs = jnp.concatenate([by_re, by_im], axis=1).astype(jnp.bfloat16)
    rhs = rhs.transpose(1, 0, 2).reshape(2 * PLANE, KX_COUNT * width)
    field = lax.dot_general(e, rhs, (((0,), (0,)), ((), ())), preferred_element_type=jnp.float32)
    field = field.reshape(rows, KX_COUNT, width) * xf.T[:, :, None]
    spectral = jnp.sum(field, axis=1)
    linear = jnp.dot(features, lin_weight, preferred_element_type=jnp.float32)
    pre = spectral / total + linear + bias[None, :]
    return jax.nn.gelu(pre, approximate=False).astype(jnp.bfloat16)


def solution(mesh):
    return jax.shard_map(
        on_device,
        mesh=mesh,
        in_specs=(
            P("pts", None),
            P(None, "pts"),
            P("pts"),
            P(),
            P(("pts", "modes"), None, None, None),
            P(),
            P(),
        ),
        out_specs=P(("pts", "modes"), None),
        check_vma=False,
    )
```

time: 506 us -> 443 us (0.88)
  the two profiles are of different devices: /device:TPU:0 before, /device:TPU:11 now
where the time goes in v1:
time: 443 us; the launch traced here: 437 us
  waiting for transfers between devices  160 us (36%)
  local copies, waits for them, and re-layouts  128 us (29%)
  matrix products  52.7 us (12%)
  other arithmetic  41.9 us (9%)
  blocking collectives  39.9 us (9%)
  between operations  14 us (3%)
    reduce_scatter x1, waiting for transfers between devices, on_device(): coef = lax.psum_scatter(coef, AXES, scatter_dimension=0, tiled=True)  122 us
    psum x1, blocking collectives, on_device(): total = lax.psum(jnp.sum(quad_weight), 'pts')  39.9 us
    all_gather x1, waiting for transfers between devices, on_device(): full = lax.all_gather(filtered, AXES, axis=0, tiled=True)  38.1 us
    gather x1, local copies, waits for them, and re-layouts, on_device(): coef = jnp.take(coef, index, axis=0, mode='clip')  33.8 us
    gather x1, local copies, waits for them, and re-layouts, on_device(): full = jnp.take(full, inverse, axis=0, mode='clip').astype(jnp.float32)  33.8 us
    transpose x1, other arithmetic, on_device(): rhs = rhs.transpose(1, 0, 2).reshape(2 * PLANE, KX_COUNT * width)  17.5 us
    dot_general x1, matrix products, on_device(): jnp.dot(e, xw.reshape(rows, KX_COUNT * width), preferred_element_type=jnp...  12.6 us
    convert_element_type x1, local copies, waits for them, and re-layouts, on_device(): (xf.T[:, :, None] * weighted.astype(jnp.float32)[:, None, :]).astype(jnp....  12.2 us
  transfers between devices with their start and end apart: 2, of which 2 were waited for; matrix products, arithmetic and copies ran while one was open for 1% of the time, Pallas kernels for 0%

profile of v1, /device:TPU:11, one launch (start us, length us, event | category | flops | bytes accessed | tf_op | source)
XLA Modules:
  0.0 437.1 jit_solution(15093316684472982699)
XLA Ops:
  6.5 0.0 copy-start
  6.5 0.0 reduce-scatter.2.cloned.1.call-start
  6.6 1.0 fusion.77
  7.5 1.0 fusion.42
  8.5 0.5 fusion.45
  9.1 2.6 subtract_convert_fusion
  11.7 4.1 copy.24
  15.8 2.6 copy.25
  18.3 4.8 %pad_maximum_fusion = bf16[1024,2048]{0,1:T(8,128)(2,1)} fusion(bf16[512,2048]{0,1:T(8,128)(2,1)} %copy.25, bf16[512,2048]{0,1:T(8,128)(2,1)} %copy.24), kind=kLoop, calls=%fused_computation.16 | loop fusion | flops 8388608 | bytes 8388608 | tf_op jit(solution)/shard_map/concatenate | solution.py:33
  23.1 6.6 %copy.26 = bf16[1024,2048]{1,0:T(8,128)(2,1)} copy(bf16[1024,2048]{0,1:T(8,128)(2,1)} %pad_maximum_fusion) | data formatting | bytes 8388608 | tf_op jit(solution)/shard_map/concatenate | solution.py:33
  29.8 0.3 fusion.56
  30.1 0.0 copy-done.3
  30.1 0.0 dynamic-slice-done
  30.1 0.3 fusion.38
  30.5 7.1 %multiply_convert_fusion = bf16[2048,16,128]{2,0,1:T(8,128)(2,1)} fusion(f32[2048,128]{1,0:T(8,128)S(1)} %fusion.38, f32[2048,16]{0,1:T(8,128)S(1)} %maximum_bitcast_fusion.2), kind=kLoop, calls=%fused_computation.3 | loop fusion | flops 8388608 | bytes 9568256 | tf_op jit(solution)/shard_map/convert_element_type | solution.py:69
  37.5 12.2 %copy.27 = bf16[2048,16,128]{0,2,1:T(8,128)(2,1)} copy(bf16[2048,16,128]{2,0,1:T(8,128)(2,1)} %multiply_convert_fusion) | data formatting | bytes 16777216 | tf_op jit(solution)/shard_map/convert_element_type | solution.py:69
  49.7 12.6 %fusion.78 = f32[2,512,2,8,128]{1,4,3,2,0:T(8,128)S(1)} fusion(bf16[2,512,2048,1,1]{2,1,4,3,0:T(8,128)(2,1)} %bitcast.107, bf16[2,8,128,2048,1]{3,2,1,0,4:T(8,128)(2,1)} %bitcast.100), kind=kOutput, calls=%fused_computation.141 | convolution fusion | flops 8589934592 | bytes 20971520 | tf_op jit(solution)/shard_map/dot_general | solution.py:70
  62.3 1.5 fusion.23
  63.8 2.2 maximum_bitcast_fusion
  66.0 6.4 %copy.28 = bf16[16,512,256]{2,1,0:T(8,128)(2,1)} copy(bf16[16,512,256]{1,2,0:T(8,128)(2,1)} %maximum_bitcast_fusion) | data formatting | bytes 8388608 | tf_op jit(solution)/shard_map/transpose | solution.py:76
  72.5 0.0 copy-done.2
  72.5 0.1 bitcast_add_fusion
  72.6 33.8 %gather_fusion = bf16[8192,256]{1,0:T(8,128)(2,1)} fusion(bf16[8192,256]{1,0:T(8,128)(2,1)} %bitcast.99, s32[8192]{0:T(1024)S(1)} %broadcast_clamp_fusion), kind=kCustom, calls=%fused_computation | custom fusion | bytes 8421376 | tf_op jit(solution)/shard_map/jit(_take)/gather | solution.py:77
  106.4 0.0 reduce-scatter.2.cloned.1.call-update
  106.4 0.3 all-gather.2.cloned.1.call-start
  106.7 122.1 %reduce-scatter.2.cloned.1.call-done = bf16[256,256]{1,0:T(8,128)(2,1)} async-done(((bf16[8192,256]{1,0:T(8,128)(2,1)}), bf16[256,256]{1,0:T(8,128)(2,1)}) %reduce-scatter.2.cloned.1.call-update) | async-done | bytes 131088 | tf_op jit(solution)/shard_map/reduce_scatter | solution.py:78
  228.8 0.9 slice_bitcast_fusion
  229.7 5.7 %fusion.6 = f32[256,1,128]{2,1,0:T(1,128)S(1)} fusion(bf16[256,2,128,128]{3,2,1,0:T(8,128)(2,1)} %param.11, bf16[256,128,1]{1,0,2:T(8,128)(2,1)S(1)} %get-tuple-element.26), kind=kOutput, calls=%fused_computation.10 | convolution fusion | flops 8388608 | bytes 8585216 | tf_op jit(solution)/shard_map/mc,mcd->md/dot_general | solution.py:83
  235.4 5.7 %fusion = f32[256,1,128]{2,1,0:T(1,128)S(1)} fusion(bf16[256,2,128,128]{3,2,1,0:T(8,128)(2,1)} %param.11, bf16[256,128,1]{1,0,2:T(8,128)(2,1)S(1)} %get-tuple-element.26), kind=kOutput, calls=%fused_computation.4 | convolution fusion | flops 8388608 | bytes 8585216 | tf_op jit(solution)/shard_map/mc,mcd->md/dot_general | solution.py:86
  241.1 5.7 %fusion.2 = f32[256,1,128]{2,1,0:T(1,128)S(1)} fusion(bf16[256,2,128,128]{3,2,1,0:T(8,128)(2,1)} %param.11, bf16[256,128,1]{1,0,2:T(8,128)(2,1)S(1)} %get-tuple-element.25), kind=kOutput, calls=%fused_computation.6 | convolution fusion | flops 8388608 | bytes 8585216 | tf_op jit(solution)/shard_map/mc,mcd->md/dot_general | solution.py:85
  246.8 5.7 %fusion.4 = f32[256,1,128]{2,1,0:T(1,128)S(1)} fusion(bf16[256,2,128,128]{3,2,1,0:T(8,128)(2,1)} %param.11, bf16[256,128,1]{1,0,2:T(8,128)(2,1)S(1)} %get-tuple-element.25), kind=kOutput, calls=%fused_computation.8 | convolution fusion | flops 8388608 | bytes 8585216 | tf_op jit(solution)/shard_map/mc,mcd->md/dot_general | solution.py:88
  252.5 0.7 pad_maximum_fusion.1
  253.2 0.0 all-gather.2.cloned.1.call-update
  253.2 0.7 reduce_sum.19
  253.9 39.9 %psum.7 = f32[]{:T(128)} all-reduce(f32[]{:T(128)} %reduce_sum.19), channel_id=1, replica_groups=mesh['pts'=16,'modes'=2] {'pts'}, use_global_device_ids=true, to_apply=%region_3.4 | all-reduce | flops 1 | bytes 8 | tf_op jit(solution)/shard_map/psum | solution.py:61
  293.8 0.3 fusion.76
  294.1 0.4 select_convert_fusion.1
  294.4 1.4 fusion.14
  295.9 38.1 %all-gather.2.cloned.1.call-done = bf16[8192,256]{1,0:T(8,128)(2,1)} async-done(((bf16[256,256]{1,0:T(8,128)(2,1)}), bf16[8192,256]{1,0:T(8,128)(2,1)}) %all-gather.2.cloned.1.call-update) | async-done | bytes 4194320 | tf_op jit(solution)/shard_map/all_gather | solution.py:90
  334.0 33.8 %gather_fusion.1 = bf16[8192,256]{1,0:T(8,128)(2,1)} fusion(bf16[8192,256]{1,0:T(8,128)(2,1)} %all-gather.2.cloned.1.call-done, s32[8192]{0:T(1024)S(1)} %fusion.72), kind=kCustom, calls=%fused_computation.1 | custom fusion | bytes 8421376 | tf_op jit(solution)/shard_map/jit(_take)/gather | solution.py:91
  367.8 9.1 %reshape.369 = f32[2,8,512,2,128]{4,3,2,1,0:T(2,128)} reshape(bf16[8192,256]{1,0:T(8,128)(2,1)} %gather_fusion.1) | data formatting | bytes 12582912 | tf_op jit(solution)/shard_map/convert_element_type | solution.py:91
  376.8 11.9 %fusion.75 = (f32[1,8,512,1,128]{4,3,2,1,0:T(1,128)S(1)}, f32[1,8,512,1,128]{4,3,2,1,0:T(1,128)S(1)}, f32[1,8,512,1,128]{4,3,2,1,0:T(1,128)S(1)}, f32[1,8,512,1,128]{4,3,2,1,0:T(1,128)S(1)}) fusion(f32[2,8,512,2,128]{4,3,2,1,0:T(2,128)} %reshape.369), kind=kLoop, calls=%fused_computation.138 | loop fusion | bytes 16777216 | tf_op jit(solution)/shard_map/slice | solution.py:94
  388.8 0.5 fusion.28
  389.3 0.5 fusion.27
  389.7 17.5 %maximum_bitcast_fusion.1 = bf16[1024,16,128]{2,0,1:T(8,128)(2,1)} fusion(bf16[8,512,128]{2,1,0:T(8,128)(2,1)S(1)} %get-tuple-element.16, bf16[8,512,128]{2,1,0:T(8,128)(2,1)S(1)} %get-tuple-element.18, bf16[8,512,128]{2,1,0:T(8,128)(2,1)S(1)} %get-tuple-element.17, bf16[8,512,128]{2,1,0:T(8,128)(2,1)S(1)} %get-tuple-element.15), kind=kLoop, calls=%fused_computation.18 | loop fusion | flops 16777216 | bytes 8388608 | tf_op jit(solution)/shard_map/transpose | solution.py:98
  407.3 6.6 %copy.33 = bf16[1024,16,128]{0,2,1:T(8,128)(2,1)} copy(bf16[1024,16,128]{2,0,1:T(8,128)(2,1)} %maximum_bitcast_fusion.1) | data formatting | bytes 8388608 | tf_op jit(solution)/shard_map/transpose | solution.py:98
  413.8 12.0 %multiply_reduce_fusion = f32[2048,128]{1,0:T(8,128)S(1)} fusion(f32[2048,16]{0,1:T(8,128)S(1)} %maximum_bitcast_fusion.2, bf16[1024,16,128]{0,2,1:T(8,128)(2,1)} %copy.33, bf16[512,2048]{0,1:T(8,128)(2,1)} %copy.25, bf16[512,2048]{0,1:T(8,128)(2,1)S(1)} %copy-done.1), kind=kOutput, calls=%fused_computation.2 | convolution fusion | flops 8606449664 | bytes 9568256 | tf_op jit(solution)/shard_map/dot_general | solution.py:99
  425.8 4.0 fusion.22
  (18 shorter events, 0.1 us)
Async XLA Ops:
  6.5 419.3 %copy-start = (bf16[128,128]{1,0:T(8,128)(2,1)S(1)}, bf16[128,128]{1,0:T(8,128)(2,1)}, u32[]{:S(2)}) copy-start(bf16[128,128]{1,0:T(8,128)(2,1)} %param.12) | copy-start | bytes 98308
  6.5 222.3 %reduce-scatter.2.cloned.1.call-start = ((), (), s32[]{:S(2)}) async-start(), calls=%async_computation.1 | async-start | bytes 4325376 | tf_op jit(solution)/shard_map/reduce_scatter | solution.py:78
  23.1 7.0 %copy-start.3 = (bf16[4096,128]{1,0:T(8,128)(2,1)S(1)}, bf16[4096,128]{1,0:T(8,128)(2,1)}, u32[]{:S(2)}) copy-start(bf16[4096,128]{1,0:T(8,128)(2,1)} %param.7) | copy-start | bytes 3145732
  23.1 7.0 %dynamic-slice-start = ((f32[4096]{0:T(1024)}, s32[]{:T(128)}), f32[2048]{0:T(1024)S(1)}, s32[]{:S(2)}) async-start(f32[4096]{0:T(1024)} %param.9, s32[]{:T(128)} %select_n.69), calls=%async_computation.3 | async-start | bytes 16896 | tf_op jit(solution)/shard_map/dynamic_slice | solution.py:64
  66.0 6.5 %copy-start.2 = (s32[3,8192]{1,0:T(4,128)S(1)}, s32[3,8192]{1,0:T(4,128)}, u32[]{:S(2)}) copy-start(s32[3,8192]{1,0:T(4,128)} %param.10) | copy-start | bytes 294916
  106.4 227.5 %all-gather.2.cloned.1.call-start = ((), (), s32[]{:S(2)}) async-start(), calls=%async_computation.2 | async-start | bytes 4325376 | tf_op jit(solution)/shard_map/all_gather | solution.py:90
  246.8 6.5 %copy-start.4 = (f32[4096]{0:T(1024)S(1)}, f32[4096]{0:T(1024)}, u32[]{:S(2)}) copy-start(f32[4096]{0:T(1024)} %param.9) | copy-start | bytes 49156
  407.3 6.6 %copy-start.1 = (bf16[512,2048]{0,1:T(8,128)(2,1)S(1)}, bf16[512,2048]{0,1:T(8,128)(2,1)}, u32[]{:S(2)}) copy-start(bf16[512,2048]{0,1:T(8,128)(2,1)} %copy.24) | copy-start | bytes 6291460
  413.8 12.0 %copy-start.5 = (f32[128]{0:T(128)S(1)}, f32[128]{0:T(128)}, u32[]{:S(2)}) copy-start(f32[128]{0:T(128)} %param.13) | copy-start | bytes 1540
Sparse Core Ops, SparseCore 0:
  106.6 122.2 reduce-scatter.1
  253.3 80.5 all-gather.1

commit v2 on v1

v2 whole, which is shorter than its diff:
```python
import math

import jax
import jax.numpy as jnp
from jax import lax
from jax.experimental import pallas as pl
from jax.experimental.pallas import tpu as pltpu
from jax.sharding import PartitionSpec as P

KX_LOW, KX_COUNT = -8, 16
KY_LOW, KY_COUNT = -8, 16
KZ_LOW, KZ_COUNT = 0, 32
HALF = KX_COUNT // 2
PLANE = KY_COUNT * KZ_COUNT
AXES = ("pts", "modes")
TAIL = 16


def cos_sin(turns):
    angle = (2.0 * math.pi) * (turns - jnp.round(turns))
    return jnp.cos(angle), jnp.sin(angle)


def factors(coords):
    x, y, z = coords[0], coords[1], coords[2]
    j = jnp.arange(HALF, dtype=jnp.float32) + 0.5
    xc, xs = cos_sin(j[:, None] * x[None, :])
    ky = jnp.arange(KY_COUNT, dtype=jnp.float32) + KY_LOW
    kz = jnp.arange(KZ_COUNT, dtype=jnp.float32) + KZ_LOW
    yc, ys = cos_sin(ky[:, None] * y[None, :])
    zc, zs = cos_sin(kz[:, None] * z[None, :] - 0.5 * x[None, :])
    return jnp.concatenate([xc, xs], axis=0).T, (yc, ys, zc, zs)


def plane_kernel(yc_ref, ys_ref, zc_ref, zs_ref, e_ref, et_ref):
    zc, zs = zc_ref[...], zs_ref[...]
    for k in range(KY_COUNT):
        yc, ys = yc_ref[pl.ds(k, 1)], ys_ref[pl.ds(k, 1)]
        re = yc * zc - ys * zs
        im = ys * zc + yc * zs
        e_ref[pl.ds(k * KZ_COUNT, KZ_COUNT)] = re.astype(jnp.bfloat16)
        e_ref[pl.ds(PLANE + k * KZ_COUNT, KZ_COUNT)] = im.astype(jnp.bfloat16)
    et_ref[...] = e_ref[...].T


def plane_factors(parts):
    rows = parts[0].shape[1]
    step = math.gcd(rows, 512)
    return pl.pallas_call(
        plane_kernel,
        grid=(rows // step,),
        out_shape=(
            jax.ShapeDtypeStruct((2 * PLANE, rows), jnp.bfloat16),
            jax.ShapeDtypeStruct((rows, 2 * PLANE), jnp.bfloat16),
        ),
        in_specs=[pl.BlockSpec((part.shape[0], step), lambda p: (0, p)) for part in parts],
        out_specs=(
            pl.BlockSpec((2 * PLANE, step), lambda p: (0, p)),
            pl.BlockSpec((step, 2 * PLANE), lambda p: (p, 0)),
        ),
        compiler_params=pltpu.CompilerParams(vmem_limit_bytes=48 << 20),
    )(*parts)


def column(table_ref, at):
    lanes = lax.broadcasted_iota(jnp.int32, table_ref.shape, 1)
    return jnp.sum(jnp.where(lanes == at, table_ref[...], 0.0), axis=1, keepdims=True)


def analyse_kernel(e_ref, xf_ref, weighted_ref, out_ref):
    j = pl.program_id(0)
    width = weighted_ref.shape[1]
    weighted = weighted_ref[...].astype(jnp.float32)
    by_cos = (column(xf_ref, j) * weighted).astype(jnp.bfloat16)
    by_sin = (column(xf_ref, HALF + j) * weighted).astype(jnp.bfloat16)
    rhs = jnp.concatenate([by_cos, by_sin], axis=1)
    re = jnp.dot(e_ref[:PLANE], rhs, preferred_element_type=jnp.float32)
    im = jnp.dot(e_ref[PLANE:], rhs, preferred_element_type=jnp.float32)
    rc, rs = re[:, :width], re[:, width:]
    ic, is_ = im[:, :width], im[:, width:]
    out_ref[0, 0, :, :width] = (rc - is_).astype(jnp.bfloat16)
    out_ref[0, 0, :, width:] = (-(ic + rs)).astype(jnp.bfloat16)
    out_ref[1, 0, :, :width] = (rc + is_).astype(jnp.bfloat16)
    out_ref[1, 0, :, width:] = (rs - ic).astype(jnp.bfloat16)


def analyse(e, xf, weighted):
    rows, width = weighted.shape
    out = pl.pallas_call(
        analyse_kernel,
        grid=(HALF,),
        out_shape=jax.ShapeDtypeStruct((2, HALF, PLANE, 2 * width), jnp.bfloat16),
        in_specs=[
            pl.BlockSpec((2 * PLANE, rows), lambda j: (0, 0)),
            pl.BlockSpec((rows, 2 * HALF), lambda j: (0, 0)),
            pl.BlockSpec((rows, width), lambda j: (0, 0)),
        ],
        out_specs=pl.BlockSpec((2, 1, PLANE, 2 * width), lambda j: (0, j, 0, 0)),
        compiler_params=pltpu.CompilerParams(vmem_limit_bytes=48 << 20),
    )(e, xf, weighted)
    return out.reshape(2 * HALF * PLANE, 2 * width)


def synthesize_kernel(et_ref, xf_ref, full_ref, out_ref):
    j = pl.program_id(0)
    width = out_ref.shape[1]
    pos = full_ref[0, 0].astype(jnp.float32)
    neg = full_ref[1, 0].astype(jnp.float32)
    pr, pi = pos[:, :width], pos[:, width:]
    nr, ni = neg[:, :width], neg[:, width:]
    top = jnp.concatenate([pr + nr, ni - pi], axis=1).astype(jnp.bfloat16)
    low = jnp.concatenate([-(pi + ni), nr - pr], axis=1).astype(jnp.bfloat16)
    field = jnp.dot(et_ref[:, :PLANE], top, preferred_element_type=jnp.float32)
    field = field + jnp.dot(et_ref[:, PLANE:], low, preferred_element_type=jnp.float32)
    add = column(xf_ref, j) * field[:, :width] + column(xf_ref, HALF + j) * field[:, width:]

    @pl.when(j == 0)
    def _():
        out_ref[...] = add

    @pl.when(j > 0)
    def _():
        out_ref[...] += add


def synthesize(et, xf, full):
    rows = et.shape[0]
    width = full.shape[1] // 2
    return pl.pallas_call(
        synthesize_kernel,
        grid=(HALF,),
        out_shape=jax.ShapeDtypeStruct((rows, width), jnp.float32),
        in_specs=[
            pl.BlockSpec((rows, 2 * PLANE), lambda j: (0, 0)),
            pl.BlockSpec((rows, 2 * HALF), lambda j: (0, 0)),
            pl.BlockSpec((2, 1, PLANE, 2 * width), lambda j: (0, j, 0, 0)),
        ],
        out_specs=pl.BlockSpec((rows, width), lambda j: (0, 0)),
        compiler_params=pltpu.CompilerParams(vmem_limit_bytes=48 << 20),
    )(et, xf, full.reshape(2, HALF, PLANE, 2 * width))


def filter_kernel(coef_ref, w_ref, out_ref):
    width = w_ref.shape[2]
    for m in range(w_ref.shape[0]):
        pair = coef_ref[m]
        by_re = jnp.dot(pair, w_ref[m, 0], preferred_element_type=jnp.float32)
        by_im = jnp.dot(pair, w_ref[m, 1], preferred_element_type=jnp.float32)
        out_ref[pl.ds(m, 1), :width] = by_re[0:1] - by_im[1:2]
        out_ref[pl.ds(m, 1), width:] = by_im[0:1] + by_re[1:2]


def filter_modes(coef, weight):
    modes, width = weight.shape[0], weight.shape[2]
    step = math.gcd(modes, 16)
    return pl.pallas_call(
        filter_kernel,
        grid=(modes // step,),
        out_shape=jax.ShapeDtypeStruct((modes, 2 * width), jnp.float32),
        in_specs=[
            pl.BlockSpec((step, 2, width), lambda m: (m, 0, 0)),
            pl.BlockSpec((step, 2, width, width), lambda m: (m, 0, 0, 0)),
        ],
        out_specs=pl.BlockSpec((step, 2 * width), lambda m: (m, 0)),
        compiler_params=pltpu.CompilerParams(vmem_limit_bytes=48 << 20),
    )(coef.reshape(modes, 2, width), weight)


def grid_index(mode_table):
    kx = mode_table[0]
    slot = jnp.where(kx >= 0, kx, HALF - 1 - kx)
    return (slot * KY_COUNT + mode_table[1] - KY_LOW) * KZ_COUNT + mode_table[2] - KZ_LOW


def inverse_index(index):
    n = index.shape[0]
    lo = 128
    hi = n // lo
    ids = jnp.arange(n, dtype=jnp.int32)
    hot_lo = (index[:, None] % lo == jnp.arange(lo)[None, :]).astype(jnp.bfloat16)
    hit = index[None, :] // lo == jnp.arange(hi)[:, None]
    top = jnp.where(hit, ids[None, :] // lo, 0).astype(jnp.bfloat16)
    low = jnp.where(hit, ids[None, :] % lo, 0).astype(jnp.bfloat16)
    got = jnp.dot(jnp.concatenate([top, low], axis=0), hot_lo, preferred_element_type=jnp.float32)
    return (got[:hi] * lo + got[hi:]).astype(jnp.int32).reshape(n)


def on_device(features, coords, quad_weight, mode_table, mode_weight, lin_weight, bias):
    width = features.shape[1]
    n_groups = lax.axis_size("modes")
    group = lax.axis_index("modes")
    rows = features.shape[0] // n_groups
    features = lax.dynamic_slice_in_dim(features, group * rows, rows, 0)
    coords = lax.dynamic_slice_in_dim(coords, group * rows, rows, 1)
    quad = lax.dynamic_slice_in_dim(quad_weight, group * rows, rows, 0)
    own = mode_weight.shape[0]
    xf, parts = factors(coords)
    e, et = plane_factors(parts)
    index = grid_index(mode_table)
    inverse = inverse_index(index)
    weighted = (quad[:, None] * features.astype(jnp.float32)).astype(jnp.bfloat16)
    coef = analyse(e, xf, weighted)
    coef = jnp.take(coef, index, axis=0, mode="clip")
    coef = lax.all_to_all(coef.reshape(-1, own, 2 * width), AXES, 0, 0)
    coef = jnp.sum(coef.astype(jnp.float32), axis=0).astype(jnp.bfloat16)
    filtered = filter_modes(coef, mode_weight).astype(jnp.bfloat16)
    share = jnp.sum(quad)
    high = lax.reduce_precision(share, 8, 7)
    mid = lax.reduce_precision(share - high, 8, 7)
    low = share - high - mid
    cells = jnp.pad(jnp.stack([high, mid, low]), (0, 2 * width - 3))
    cells = jnp.broadcast_to(cells[None], (TAIL, 2 * width)).astype(jnp.bfloat16)
    sent = jnp.concatenate([filtered, cells], axis=0)
    full = lax.all_gather(sent, AXES, axis=0, tiled=True)
    devices = full.shape[0] // (own + TAIL)
    shares = full.reshape(devices, own + TAIL, 2 * width)[:, own, :3]
    total = jnp.sum(shares.astype(jnp.float32))
    full = jnp.take(full, inverse + inverse // own * TAIL, axis=0, mode="clip")
    spectral = synthesize(et, xf, full)
    linear = jnp.dot(features, lin_weight, preferred_element_type=jnp.float32)
    pre = spectral / total + linear + bias[None, :]
    return jax.nn.gelu(pre, approximate=False).astype(jnp.bfloat16)


def solution(mesh):
    return jax.shard_map(
        on_device,
        mesh=mesh,
        in_specs=(
            P("pts", None),
            P(None, "pts"),
            P("pts"),
            P(),
            P(("pts", "modes"), None, None, None),
            P(),
            P(),
        ),
        out_specs=P(("pts", "modes"), None),
        check_vma=False,
    )
```

time: 443 us -> 309 us (0.70)
  local copies, waits for them, and re-layouts: 128 us -> 71.6 us
  matrix products: 52.7 us -> 5.31 us
  Pallas kernels: 0 us -> 44.5 us
  blocking collectives: 39.9 us -> 0 us
  other arithmetic: 41.9 us -> 12.5 us
  waiting for transfers between devices: 160 us -> 148 us
  starting transfers between devices: 0.26 us -> 6.57 us
    reduce_scatter x1 -> x0, waiting for transfers between devices: 122 us -> none  [on_device(): coef = lax.psum_scatter(coef, AXES, scatter_dimension=0, tiled=True)]
    all_to_all x0 -> x1, waiting for transfers between devices: none -> 85.6 us  [on_device(): coef = lax.all_to_all(coef.reshape(-1, own, 2 * width), AXES, 0, 0)]
    dot_general x6 -> x0, matrix products: 47.3 us -> none  [the longest x1 12.6 us: on_device(): jnp.dot(e, xw.reshape(rows, KX_COUNT * width), preferred_element_type=jnp...]
    pallas_call x0 -> x4, Pallas kernels: none -> 44.5 us  [the longest x1 13.9 us: filter_modes(): pl.pallas_call(filter_kernel, grid=(modes // step,), out_shape=jax.ShapeD...]
    psum x1 -> x0, blocking collectives: 39.9 us -> none  [on_device(): total = lax.psum(jnp.sum(quad_weight), 'pts')]
    all_gather x1, waiting for transfers between devices: 38.1 us -> 62.4 us  [on_device(): full = lax.all_gather(sent, AXES, axis=0, tiled=True)]
    convert_element_type x2 -> x0, local copies, waits for them, and re-layouts: 21.3 us -> none  [the longest x1 12.2 us: on_device(): (xf.T[:, :, None] * weighted.astype(jnp.float32)[:, None, :]).astype(jnp....]
    transpose x3 -> x0, other arithmetic: 19.8 us -> none  [the longest x1 17.5 us: on_device(): rhs = rhs.transpose(1, 0, 2).reshape(2 * PLANE, KX_COUNT * width)]
where the time goes in v2:
time: 309 us; the launch traced here: 307 us
  waiting for transfers between devices  148 us (48%)
  local copies, waits for them, and re-layouts  71.6 us (23%)
  Pallas kernels  44.5 us (14%)
  between operations  18.4 us (6%)
  other arithmetic  12.5 us (4%)
  starting transfers between devices  6.57 us (2%)
  matrix products  5.31 us (2%)
    all_to_all x1, waiting for transfers between devices, on_device(): coef = lax.all_to_all(coef.reshape(-1, own, 2 * width), AXES, 0, 0)  85.6 us
    all_gather x1, waiting for transfers between devices, on_device(): full = lax.all_gather(sent, AXES, axis=0, tiled=True)  62.4 us
    gather x1, local copies, waits for them, and re-layouts, on_device(): full = jnp.take(full, inverse + inverse // own * TAIL, axis=0, mode='clip')  33.7 us
    gather x1, local copies, waits for them, and re-layouts, on_device(): coef = jnp.take(coef, index, axis=0, mode='clip')  33.6 us
    pallas_call x1, Pallas kernels, filter_modes(): pl.pallas_call(filter_kernel, grid=(modes // step,), out_shape=jax.ShapeD...  13.9 us
    pallas_call x1, Pallas kernels, analyse(): pl.pallas_call(analyse_kernel, grid=(HALF,), out_shape=jax.ShapeDtypeStru...  13.5 us
    pallas_call x1, Pallas kernels, synthesize(): pl.pallas_call(synthesize_kernel, grid=(HALF,), out_shape=jax.ShapeDtypeS...  13.5 us
    all_to_all x1, starting transfers between devices, on_device(): coef = lax.all_to_all(coef.reshape(-1, own, 2 * width), AXES, 0, 0)  6.35 us
  transfers between devices with their start and end apart: 2, of which 2 were waited for; matrix products, arithmetic and copies ran while one was open for 1% of the time, Pallas kernels for 0%

profile of v2, /device:TPU:11, one launch (start us, length us, event | category | flops | bytes accessed | tf_op | source)
XLA Modules:
  0.0 307.0 jit_solution(7974833676617333465)
XLA Ops:
  6.5 0.0 copy-start
  6.6 1.2 bitcast_add_fusion
  7.7 1.3 fusion.52
  9.0 1.0 fusion.54
  10.0 0.3 fusion.29
  10.4 0.3 copy.8
  10.7 0.5 fusion.21
  11.2 1.0 fusion.18
  12.2 1.4 multiply_convert_fusion.weighted_ref
  13.6 3.6 %shard_map.73 = (bf16[1024,2048]{1,0:T(8,128)(2,1)S(1)}, bf16[2048,1024]{1,0:T(8,128)(2,1)}) custom-call(f32[16,2048]{1,0:T(8,128)S(1)} %get-tuple-element.28.yc_ref, f32[16,2048]{1,0:T(8,128)S(1)} %get-tuple-element.27.ys_ref, f32[32,2048]{1,0:T(8,128)S(1)} %get-tuple-element.24.zc_ref, f32[32,2048]{1,0:T(8,128)S(1)} %get-tuple-element.23.zs_ref), custom_call_target="tpu_custom_call" | custom-call | tf_op jit(solution)/shard_map/pallas_call | solution.py:49
  17.2 0.0 copy-start.2
  17.2 2.0 copy-done.2
  19.1 13.5 %shard_map.74 = bf16[2,8,512,256]{3,2,1,0:T(8,128)(2,1)S(1)} custom-call(bf16[1024,2048]{1,0:T(8,128)(2,1)} %copy-done.2, f32[2048,16]{1,0:T(8,128)S(1)} %bitcast.31, bf16[2048,128]{1,0:T(8,128)(2,1)S(1)} %multiply_convert_fusion.weighted_ref), custom_call_target="tpu_custom_call" | custom-call | tf_op jit(solution)/shard_map/pallas_call | solution.py:89
  32.7 0.0 copy-start.1
  32.7 2.0 copy-done.1
  34.6 33.6 %gather_fusion = bf16[8192,256]{1,0:T(8,128)(2,1)} fusion(bf16[8192,256]{1,0:T(8,128)(2,1)} %bitcast.30, s32[8192]{0:T(1024)S(1)} %broadcast_clamp_fusion.1), kind=kCustom, calls=%fused_computation | custom fusion | bytes 8421376 | tf_op jit(solution)/shard_map/jit(_take)/gather | solution.py:203
  68.3 6.4 %all-to-all-start = ((bf16[32,256,256]{2,1,0:T(8,128)(2,1)}), bf16[32,256,256]{2,1,0:T(8,128)(2,1)}, u32[]{:S(2)}, u32[]{:S(2)}) async-start(bf16[32,256,256]{2,1,0:T(8,128)(2,1)} %bitcast.34), calls=%async_computation | async-start | bytes 8388608 | tf_op jit(solution)/shard_map/all_to_all | solution.py:204
  74.6 0.2 all-gather.2.cloned.1.call-start
  79.6 0.1 fusion.49
  79.7 85.6 %all-to-all-done = bf16[32,256,256]{2,1,0:T(8,128)(2,1)} async-done(((bf16[32,256,256]{2,1,0:T(8,128)(2,1)}), bf16[32,256,256]{2,1,0:T(8,128)(2,1)}, u32[]{:S(2)}, u32[]{:S(2)}) %all-to-all-start) | async-done | bytes 4194336 | tf_op jit(solution)/shard_map/all_to_all | solution.py:204
  165.3 2.8 reduce_sum.30
  168.1 0.0 copy-start.3
  168.1 13.9 %shard_map.75 = f32[256,256]{1,0:T(8,128)S(1)} custom-call(bf16[256,2,128]{2,1,0:T(2,128)(2,1)S(1)} %reshape.271.coef_ref, bf16[256,2,128,128]{3,2,1,0:T(8,128)(2,1)} %w_ref.1), custom_call_target="tpu_custom_call" | custom-call | tf_op jit(solution)/shard_map/pallas_call | solution.py:156
  182.0 0.7 pad_maximum_fusion
  182.7 0.0 all-gather.2.cloned.1.call-update
  182.7 0.0 copy-done.3
  182.8 0.3 fusion.53
  183.1 0.4 select_convert_fusion.1
  183.4 1.4 fusion
  184.9 0.2 multiply_add_fusion
  185.1 62.4 %all-gather.2.cloned.1.call-done = bf16[8704,256]{1,0:T(8,128)(2,1)} async-done(((bf16[272,256]{1,0:T(8,128)(2,1)}), bf16[8704,256]{1,0:T(8,128)(2,1)}) %all-gather.2.cloned.1.call-update) | async-done | bytes 4456464 | tf_op jit(solution)/shard_map/all_gather | solution.py:214
  247.5 1.5 fusion.44
  249.0 33.7 %gather_fusion.1 = bf16[8192,256]{1,0:T(8,128)(2,1)} fusion(bf16[8704,256]{1,0:T(8,128)(2,1)} %all-gather.2.cloned.1.call-done, s32[8192]{0:T(1024)S(1)} %broadcast_clamp_fusion), kind=kCustom, calls=%fused_computation.1 | custom fusion | bytes 8421376 | tf_op jit(solution)/shard_map/jit(_take)/gather | solution.py:218
  282.7 0.0 copy-start.4
  282.7 0.0 copy-start.5
  282.7 13.5 %shard_map.76 = f32[2048,128]{1,0:T(8,128)S(1)} custom-call(bf16[2048,1024]{1,0:T(8,128)(2,1)} %get-tuple-element.7.et_ref, f32[2048,16]{1,0:T(8,128)S(1)} %bitcast.32, bf16[2,8,512,256]{3,2,1,0:T(8,128)(2,1)} %bitcast.35), custom_call_target="tpu_custom_call" | custom-call | tf_op jit(solution)/shard_map/pallas_call | solution.py:129
  296.2 0.0 copy-done
  296.2 0.0 copy-done.4
  296.2 0.0 copy-done.5
  296.2 3.9 %fusion.8 = bf16[2048,128]{1,0:T(8,128)(2,1)} fusion(bf16[128,128]{1,0:T(8,128)(2,1)S(1)} %copy-done, f32[2048,128]{1,0:T(8,128)S(1)} %shard_map.76, f32[128]{0:T(128)S(1)} %copy-done.5, f32[]{:T(128)} %fusion.44, bf16[4096,128]{1,0:T(8,128)(2,1)S(1)} %copy-done.4, s32[]{:T(128)S(6)} %select_n.80), kind=kOutput, calls=%fused_computation.16 | convolution fusion | flops 84934656 | bytes 2130440 | tf_op jit(solution)/shard_map/dot_general | solution.py:220
  (11 shorter events, 0.2 us)
Async XLA Ops:
  6.5 289.7 %copy-start = (bf16[128,128]{1,0:T(8,128)(2,1)S(1)}, bf16[128,128]{1,0:T(8,128)(2,1)}, u32[]{:S(2)}) copy-start(bf16[128,128]{1,0:T(8,128)(2,1)} %param.12) | copy-start | bytes 98308
  17.2 2.0 copy-start.2
  32.7 2.0 copy-start.1
  68.3 97.0 %all-to-all-start = ((bf16[32,256,256]{2,1,0:T(8,128)(2,1)}), bf16[32,256,256]{2,1,0:T(8,128)(2,1)}, u32[]{:S(2)}, u32[]{:S(2)}) async-start(bf16[32,256,256]{2,1,0:T(8,128)(2,1)} %bitcast.34), calls=%async_computation | async-start | bytes 8388608 | tf_op jit(solution)/shard_map/all_to_all | solution.py:204
  74.6 172.9 %all-gather.2.cloned.1.call-start = ((), (), s32[]{:S(2)}) async-start(), calls=%async_computation.1 | async-start | bytes 4595712 | tf_op jit(solution)/shard_map/all_gather | solution.py:214
  168.1 14.7 %copy-start.3 = (s32[3,8192]{1,0:T(4,128)S(1)}, s32[3,8192]{1,0:T(4,128)}, u32[]{:S(2)}) copy-start(s32[3,8192]{1,0:T(4,128)} %param.10) | copy-start | bytes 294916
  282.7 13.5 %copy-start.4 = (bf16[4096,128]{1,0:T(8,128)(2,1)S(1)}, bf16[4096,128]{1,0:T(8,128)(2,1)}, u32[]{:S(2)}) copy-start(bf16[4096,128]{1,0:T(8,128)(2,1)} %param.7) | copy-start | bytes 3145732
  282.7 13.5 %copy-start.5 = (f32[128]{0:T(128)S(1)}, f32[128]{0:T(128)}, u32[]{:S(2)}) copy-start(f32[128]{0:T(128)} %param.13) | copy-start | bytes 1540
Sparse Core Ops, SparseCore 0:
  182.9 64.5 all-gather.1

commit v3 on v2

--- a/solution.py
+++ b/solution.py
@@ -5,6 +5,7 @@
 from jax import lax
 from jax.experimental import pallas as pl
 from jax.experimental.pallas import tpu as pltpu
+from jax.sharding import Mesh
 from jax.sharding import PartitionSpec as P
 
 KX_LOW, KX_COUNT = -8, 16
@@ -12,7 +13,8 @@
 KZ_LOW, KZ_COUNT = 0, 32
 HALF = KX_COUNT // 2
 PLANE = KY_COUNT * KZ_COUNT
-AXES = ("pts", "modes")
+PTS = ("chip", "core")
+AXES = PTS + ("modes",)
 TAIL = 16
 
 
@@ -166,6 +168,48 @@
     )(coef.reshape(modes, 2, width), weight)
 
 
+def take_kernel(index_ref, src_ref, out_ref, wide, picked):
+    @pl.when(pl.program_id(0) == 0)
+    def _():
+        wide[...] = src_ref[...].astype(jnp.float32)
+
+    rows = out_ref.shape[0]
+    base = pl.program_id(0) * rows
+    unroll = math.gcd(rows, 16)
+
+    def body(block, carry):
+        at = block * unroll
+        sources = [index_ref[base + at + k] for k in range(unroll)]
+        found = [wide[pl.ds(source, 1), :] for source in sources]
+        start = pl.multiple_of(at, unroll)
+        picked[pl.ds(start, unroll), :] = jnp.concatenate(found, axis=0)
+        return carry
+
+    lax.fori_loop(0, rows // unroll, body, 0)
+    out_ref[...] = picked[...].astype(out_ref.dtype)
+
+
+def take_rows(table, index):
+    n, width = table.shape
+    m = index.shape[0]
+    step = math.gcd(m, 512)
+    return pl.pallas_call(
+        take_kernel,
+        out_shape=jax.ShapeDtypeStruct((m, width), table.dtype),
+        grid_spec=pltpu.PrefetchScalarGridSpec(
+            num_scalar_prefetch=1,
+            grid=(m // step,),
+            in_specs=[pl.BlockSpec((n, width), lambda b, index: (0, 0))],
+            out_specs=pl.BlockSpec((step, width), lambda b, index: (b, 0)),
+            scratch_shapes=[
+                pltpu.VMEM((n, width), jnp.float32),
+                pltpu.VMEM((step, width), jnp.float32),
+            ],
+        ),
+        compiler_params=pltpu.CompilerParams(vmem_limit_bytes=48 << 20),
+    )(index, table)
+
+
 def grid_index(mode_table):
     kx = mode_table[0]
     slot = jnp.where(kx >= 0, kx, HALF - 1 - kx)
@@ -200,8 +244,14 @@
     inverse = inverse_index(index)
     weighted = (quad[:, None] * features.astype(jnp.float32)).astype(jnp.bfloat16)
     coef = analyse(e, xf, weighted)
-    coef = jnp.take(coef, index, axis=0, mode="clip")
-    coef = lax.all_to_all(coef.reshape(-1, own, 2 * width), AXES, 0, 0)
+    coef = take_rows(coef, index)
+    core = lax.axis_index("core")
+    halves = coef.reshape(-1, 2, n_groups, own, 2 * width)
+    away = lax.dynamic_index_in_dim(halves, 1 - core, 1, False)
+    home = lax.dynamic_index_in_dim(halves, core, 1, False)
+    came = lax.ppermute(away, "core", [(0, 1), (1, 0)])
+    both = (home.astype(jnp.float32) + came.astype(jnp.float32)).astype(jnp.bfloat16)
+    coef = lax.all_to_all(both.reshape(-1, own, 2 * width), ("chip", "modes"), 0, 0)
     coef = jnp.sum(coef.astype(jnp.float32), axis=0).astype(jnp.bfloat16)
     filtered = filter_modes(coef, mode_weight).astype(jnp.bfloat16)
     share = jnp.sum(quad)
@@ -215,7 +265,7 @@
     devices = full.shape[0] // (own + TAIL)
     shares = full.reshape(devices, own + TAIL, 2 * width)[:, own, :3]
     total = jnp.sum(shares.astype(jnp.float32))
-    full = jnp.take(full, inverse + inverse // own * TAIL, axis=0, mode="clip")
+    full = take_rows(full, inverse + inverse // own * TAIL)
     spectral = synthesize(et, xf, full)
     linear = jnp.dot(features, lin_weight, preferred_element_type=jnp.float32)
     pre = spectral / total + linear + bias[None, :]
@@ -223,18 +273,20 @@
 
 
 def solution(mesh):
+    shape = (mesh.shape["pts"] // 2, 2, mesh.shape["modes"])
+    mesh = Mesh(mesh.devices.reshape(shape), AXES)
     return jax.shard_map(
         on_device,
         mesh=mesh,
         in_specs=(
-            P("pts", None),
-            P(None, "pts"),
-            P("pts"),
+            P(PTS, None),
+            P(None, PTS),
+            P(PTS),
             P(),
-            P(("pts", "modes"), None, None, None),
+            P(AXES, None, None, None),
             P(),
             P(),
         ),
-        out_specs=P(("pts", "modes"), None),
+        out_specs=P(AXES, None),
         check_vma=False,
     )

time: 309 us -> 252 us (0.82)
  local copies, waits for them, and re-layouts: 71.6 us -> 8.96 us
  Pallas kernels: 44.5 us -> 89 us
  waiting for transfers between devices: 148 us -> 108 us
    gather x2 -> x0, local copies, waits for them, and re-layouts: 67.3 us -> none  [the longest x1 33.7 us: on_device(): full = jnp.take(full, inverse + inverse // own * TAIL, axis=0, mode='clip')]
    pallas_call x0 -> x2, Pallas kernels: none -> 44.6 us  [take_rows(): pl.pallas_call(take_kernel, out_shape=jax.ShapeDtypeStruct((m, width), ta...]
    all_to_all x1, waiting for transfers between devices: 85.6 us -> 42.9 us  [on_device(): lax.all_to_all(both.reshape(-1, own, 2 * width), ('chip', 'modes'), 0, 0)]
    ppermute x0 -> x1, waiting for transfers between devices: none -> 4 us  [on_device(): came = lax.ppermute(away, 'core', [(0, 1), (1, 0)])]
    convert_element_type x1, other arithmetic: 0.01 us -> 3.56 us  [on_device(): (home.astype(jnp.float32) + came.astype(jnp.float32)).astype(jnp.bfloat16)]
    unnamed x12 -> x16, local copies, waits for them, and re-layouts: 3.94 us -> 6.92 us
  transfers between devices with their start and end apart: 2 -> 3, of which waited for: 2 -> 3; matrix products, arithmetic and copies ran while one was open for 1% -> 1% of each run, Pallas kernels for 0% -> 0%
where the time goes in v3:
time: 252 us; the launch traced here: 250 us
  waiting for transfers between devices  108 us (43%)
  Pallas kernels  89 us (35%)
  between operations  18.5 us (7%)
  other arithmetic  12.4 us (5%)
  local copies, waits for them, and re-layouts  8.96 us (4%)
  starting transfers between devices  7.53 us (3%)
  matrix products  5.32 us (2%)
    all_gather x1, waiting for transfers between devices, on_device(): full = lax.all_gather(sent, AXES, axis=0, tiled=True)  61.3 us
    pallas_call x2, Pallas kernels, take_rows(): pl.pallas_call(take_kernel, out_shape=jax.ShapeDtypeStruct((m, width), ta...  44.6 us
    all_to_all x1, waiting for transfers between devices, on_device(): lax.all_to_all(both.reshape(-1, own, 2 * width), ('chip', 'modes'), 0, 0)  42.9 us
    pallas_call x1, Pallas kernels, filter_modes(): pl.pallas_call(filter_kernel, grid=(modes // step,), out_shape=jax.ShapeD...  13.9 us
    pallas_call x1, Pallas kernels, analyse(): pl.pallas_call(analyse_kernel, grid=(HALF,), out_shape=jax.ShapeDtypeStru...  13.5 us
    pallas_call x1, Pallas kernels, synthesize(): pl.pallas_call(synthesize_kernel, grid=(HALF,), out_shape=jax.ShapeDtypeS...  13.5 us
    unnamed x16, local copies, waits for them, and re-layouts  6.92 us
    all_to_all x1, starting transfers between devices, on_device(): lax.all_to_all(both.reshape(-1, own, 2 * width), ('chip', 'modes'), 0, 0)  6.64 us
  transfers between devices with their start and end apart: 3, of which 3 were waited for; matrix products, arithmetic and copies ran while one was open for 1% of the time, Pallas kernels for 0%

profile of v3, /device:TPU:11, one launch (start us, length us, event | category | flops | bytes accessed | tf_op | source)
XLA Modules:
  0.0 250.0 jit_solution(13951250791775278781)
XLA Ops:
  6.5 0.0 copy-start
  6.5 0.0 copy-start.5
  6.6 1.4 fusion.58
  7.9 1.3 fusion.56
  9.2 1.0 fusion.59
  10.2 0.3 fusion.30
  10.6 0.3 copy.8
  10.9 0.5 fusion.22
  11.5 1.0 fusion.19
  12.4 0.0 copy-done.5
  12.4 0.3 multiply_convert_fusion.weighted_ref
  12.8 3.5 %shard_map.73 = (bf16[1024,2048]{1,0:T(8,128)(2,1)S(1)}, bf16[2048,1024]{1,0:T(8,128)(2,1)}) custom-call(f32[16,2048]{1,0:T(8,128)S(1)} %get-tuple-element.30.yc_ref, f32[16,2048]{1,0:T(8,128)S(1)} %get-tuple-element.29.ys_ref, f32[32,2048]{1,0:T(8,128)S(1)} %get-tuple-element.26.zc_ref, f32[32,2048]{1,0:T(8,128)S(1)} %get-tuple-element.25.zs_ref), custom_call_target="tpu_custom_call" | custom-call | tf_op jit(solution)/shard_map/pallas_call | solution.py:51
  16.3 0.0 copy-start.4
  16.3 2.0 copy-done.4
  18.3 13.5 %shard_map.74 = bf16[2,8,512,256]{3,2,1,0:T(8,128)(2,1)S(1)} custom-call(bf16[1024,2048]{1,0:T(8,128)(2,1)} %copy-done.4, f32[2048,16]{1,0:T(8,128)S(1)} %bitcast.31, bf16[2048,128]{1,0:T(8,128)(2,1)S(1)} %multiply_convert_fusion.weighted_ref), custom_call_target="tpu_custom_call" | custom-call | tf_op jit(solution)/shard_map/pallas_call | solution.py:91
  31.8 0.0 copy-start.3
  31.8 2.0 copy-done.3
  33.8 22.3 %shard_map.75 = bf16[8192,256]{1,0:T(8,128)(2,1)S(1)} custom-call(s32[8192]{0:T(1024)S(1)} %get-tuple-element.12.index_ref, bf16[8192,256]{1,0:T(8,128)(2,1)} %bitcast.30), custom_call_target="tpu_custom_call" | custom-call | tf_op jit(solution)/shard_map/pallas_call | solution.py:196
  56.0 0.0 copy-start.1
  56.1 1.7 dynamic-slice_bitcast_fusion
  57.7 1.0 copy-done.1
  58.7 0.7 collective-permute-start
  59.4 4.0 %collective-permute-done = bf16[8,2,256,256]{3,2,1,0:T(8,128)(2,1)S(1)} collective-permute-done((bf16[8,2,256,256]{3,2,1,0:T(8,128)(2,1)}, bf16[8,2,256,256]{3,2,1,0:T(8,128)(2,1)S(1)}, u32[]{:S(2)}, u32[]{:S(2)}) %collective-permute-start) | collective-permute-done | bytes 2097184 | tf_op jit(solution)/shard_map/ppermute | solution.py:252
  63.4 3.6 %fusion = bf16[8,2,256,256]{3,2,1,0:T(8,128)(2,1)} fusion(bf16[8,2,256,256]{3,2,1,0:T(8,128)(2,1)S(1)} %collective-permute-done, bf16[8,2,2,256,256]{4,3,2,1,0:T(8,128)(2,1)} %bitcast.28, s32[]{:T(128)S(6)} %select_n.82), kind=kLoop, calls=%fused_computation.1 | loop fusion | flops 4194304 | bytes 6291460 | tf_op jit(solution)/shard_map/convert_element_type | solution.py:253
  67.0 6.6 %all-to-all-start = ((bf16[16,256,256]{2,1,0:T(8,128)(2,1)}), bf16[16,256,256]{2,1,0:T(8,128)(2,1)S(1)}, u32[]{:S(2)}, u32[]{:S(2)}) async-start(bf16[16,256,256]{2,1,0:T(8,128)(2,1)} %bitcast.14), calls=%async_computation | async-start | bytes 4194304 | tf_op jit(solution)/shard_map/all_to_all | solution.py:254
  73.6 0.2 all-gather.2.cloned.1.call-start
  78.7 0.1 fusion.54
  78.8 42.9 %all-to-all-done = bf16[16,256,256]{2,1,0:T(8,128)(2,1)S(1)} async-done(((bf16[16,256,256]{2,1,0:T(8,128)(2,1)}), bf16[16,256,256]{2,1,0:T(8,128)(2,1)S(1)}, u32[]{:S(2)}, u32[]{:S(2)}) %all-to-all-start) | async-done | bytes 2097184 | tf_op jit(solution)/shard_map/all_to_all | solution.py:254
  121.7 0.3 reduce_sum.30
  122.1 13.9 %shard_map.76 = f32[256,256]{1,0:T(8,128)S(1)} custom-call(bf16[256,2,128]{2,1,0:T(2,128)(2,1)S(1)} %reshape.152.coef_ref, bf16[256,2,128,128]{3,2,1,0:T(8,128)(2,1)} %w_ref.1), custom_call_target="tpu_custom_call" | custom-call | tf_op jit(solution)/shard_map/pallas_call | solution.py:158
  136.0 0.7 pad_maximum_fusion
  136.6 0.0 all-gather.2.cloned.1.call-update
  136.7 0.4 select_convert_fusion.1
  137.0 1.4 fusion.1
  138.5 61.3 %all-gather.2.cloned.1.call-done.src_ref = bf16[8704,256]{1,0:T(8,128)(2,1)} async-done(((bf16[272,256]{1,0:T(8,128)(2,1)}), bf16[8704,256]{1,0:T(8,128)(2,1)}) %all-gather.2.cloned.1.call-update) | async-done | bytes 4456464 | tf_op jit(solution)/shard_map/all_gather | solution.py:264
  199.8 1.5 fusion.48
  201.3 22.4 %shard_map.77 = bf16[8192,256]{1,0:T(8,128)(2,1)S(1)} custom-call(s32[8192]{0:T(1024)S(1)} %fusion.36.index_ref, bf16[8704,256]{1,0:T(8,128)(2,1)} %all-gather.2.cloned.1.call-done.src_ref), custom_call_target="tpu_custom_call" | custom-call | tf_op jit(solution)/shard_map/pallas_call | solution.py:196
  223.7 0.0 copy-start.2
  223.7 2.0 copy-done.2
  225.7 0.0 copy-start.6
  225.7 0.0 copy-start.7
  225.7 13.5 %shard_map.78 = f32[2048,128]{1,0:T(8,128)S(1)} custom-call(bf16[2048,1024]{1,0:T(8,128)(2,1)} %get-tuple-element.7.et_ref, f32[2048,16]{1,0:T(8,128)S(1)} %bitcast.32, bf16[2,8,512,256]{3,2,1,0:T(8,128)(2,1)} %bitcast.29), custom_call_target="tpu_custom_call" | custom-call | tf_op jit(solution)/shard_map/pallas_call | solution.py:131
  239.2 0.0 copy-done
  239.2 0.0 copy-done.6
  239.2 0.0 copy-done.7
  239.2 3.9 %fusion.9 = bf16[2048,128]{1,0:T(8,128)(2,1)} fusion(bf16[128,128]{1,0:T(8,128)(2,1)S(1)} %copy-done, f32[2048,128]{1,0:T(8,128)S(1)} %shard_map.78, f32[128]{0:T(128)S(1)} %copy-done.7, f32[]{:T(128)} %fusion.48, bf16[4096,128]{1,0:T(8,128)(2,1)S(1)} %copy-done.6, s32[]{:T(128)S(6)} %select_n.72), kind=kOutput, calls=%fused_computation.17 | convolution fusion | flops 84934656 | bytes 2130440 | tf_op jit(solution)/shard_map/dot_general | solution.py:270
  (9 shorter events, 0.2 us)
Async XLA Ops:
  6.5 232.6 %copy-start = (bf16[128,128]{1,0:T(8,128)(2,1)S(1)}, bf16[128,128]{1,0:T(8,128)(2,1)}, u32[]{:S(2)}) copy-start(bf16[128,128]{1,0:T(8,128)(2,1)} %param.12) | copy-start | bytes 98308
  6.5 5.9 %copy-start.5 = (bf16[4096,128]{1,0:T(8,128)(2,1)S(1)}, bf16[4096,128]{1,0:T(8,128)(2,1)}, u32[]{:S(2)}) copy-start(bf16[4096,128]{1,0:T(8,128)(2,1)} %param.7) | copy-start | bytes 3145732
  16.3 2.0 copy-start.4
  31.8 2.0 copy-start.3
  56.0 2.7 %copy-start.1 = (bf16[8192,256]{1,0:T(8,128)(2,1)}, bf16[8192,256]{1,0:T(8,128)(2,1)S(1)}, u32[]{:S(2)}) copy-start(bf16[8192,256]{1,0:T(8,128)(2,1)S(1)} %shard_map.75) | copy-start | bytes 12582916
  58.7 4.7 %collective-permute-start = (bf16[8,2,256,256]{3,2,1,0:T(8,128)(2,1)}, bf16[8,2,256,256]{3,2,1,0:T(8,128)(2,1)S(1)}, u32[]{:S(2)}, u32[]{:S(2)}) collective-permute-start(bf16[8,2,256,256]{3,2,1,0:T(8,128)(2,1)} %dynamic-slice_bitcast_fusion), channel_id=1, source_target_pairs={{0,2},{2,0},{1,3},{3,1},{4,6},{6,4},{5,7},{7,5},{8,10},{10,8},{9,1... | collective-permute-start | bytes 6291464 | tf_op jit(solution)/shard_map/ppermute | solution.py:252
  67.0 54.8 %all-to-all-start = ((bf16[16,256,256]{2,1,0:T(8,128)(2,1)}), bf16[16,256,256]{2,1,0:T(8,128)(2,1)S(1)}, u32[]{:S(2)}, u32[]{:S(2)}) async-start(bf16[16,256,256]{2,1,0:T(8,128)(2,1)} %bitcast.14), calls=%async_computation | async-start | bytes 4194304 | tf_op jit(solution)/shard_map/all_to_all | solution.py:254
  73.6 126.2 %all-gather.2.cloned.1.call-start = ((), (), s32[]{:S(2)}) async-start(), calls=%async_computation.1 | async-start | bytes 4595712 | tf_op jit(solution)/shard_map/all_gather | solution.py:264
  223.7 2.0 copy-start.2
  225.7 13.5 %copy-start.6 = (bf16[4096,128]{1,0:T(8,128)(2,1)S(1)}, bf16[4096,128]{1,0:T(8,128)(2,1)}, u32[]{:S(2)}) copy-start(bf16[4096,128]{1,0:T(8,128)(2,1)} %param.7) | copy-start | bytes 3145732
  225.7 13.5 %copy-start.7 = (f32[128]{0:T(128)S(1)}, f32[128]{0:T(128)}, u32[]{:S(2)}) copy-start(f32[128]{0:T(128)} %param.13) | copy-start | bytes 1540
Sparse Core Ops, SparseCore 0:
  136.8 62.9 all-gather.1

commit v4 on v3

--- a/solution.py
+++ b/solution.py
@@ -168,10 +168,14 @@
     )(coef.reshape(modes, 2, width), weight)
 
 
-def take_kernel(index_ref, src_ref, out_ref, wide, picked):
+def take_kernel(index_ref, *refs):
+    *src_refs, out_ref, wide, picked = refs
+
     @pl.when(pl.program_id(0) == 0)
     def _():
-        wide[...] = src_ref[...].astype(jnp.float32)
+        for i, src_ref in enumerate(src_refs):
+            n = src_ref.shape[0]
+            wide[i * n : (i + 1) * n] = src_ref[...].astype(jnp.float32)
 
     rows = out_ref.shape[0]
     base = pl.program_id(0) * rows
@@ -189,25 +193,25 @@
     out_ref[...] = picked[...].astype(out_ref.dtype)
 
 
-def take_rows(table, index):
-    n, width = table.shape
+def take_rows(tables, index):
+    n, width = tables[0].shape
     m = index.shape[0]
     step = math.gcd(m, 512)
     return pl.pallas_call(
         take_kernel,
-        out_shape=jax.ShapeDtypeStruct((m, width), table.dtype),
+        out_shape=jax.ShapeDtypeStruct((m, width), tables[0].dtype),
         grid_spec=pltpu.PrefetchScalarGridSpec(
             num_scalar_prefetch=1,
             grid=(m // step,),
-            in_specs=[pl.BlockSpec((n, width), lambda b, index: (0, 0))],
+            in_specs=[pl.BlockSpec((n, width), lambda b, index: (0, 0)) for _ in tables],
             out_specs=pl.BlockSpec((step, width), lambda b, index: (b, 0)),
             scratch_shapes=[
-                pltpu.VMEM((n, width), jnp.float32),
+                pltpu.VMEM((len(tables) * n, width), jnp.float32),
                 pltpu.VMEM((step, width), jnp.float32),
             ],
         ),
         compiler_params=pltpu.CompilerParams(vmem_limit_bytes=48 << 20),
-    )(index, table)
+    )(index, *tables)
 
 
 def grid_index(mode_table):
@@ -244,7 +248,7 @@
     inverse = inverse_index(index)
     weighted = (quad[:, None] * features.astype(jnp.float32)).astype(jnp.bfloat16)
     coef = analyse(e, xf, weighted)
-    coef = take_rows(coef, index)
+    coef = take_rows([coef], index)
     core = lax.axis_index("core")
     halves = coef.reshape(-1, 2, n_groups, own, 2 * width)
     away = lax.dynamic_index_in_dim(halves, 1 - core, 1, False)
@@ -261,11 +265,19 @@
     cells = jnp.pad(jnp.stack([high, mid, low]), (0, 2 * width - 3))
     cells = jnp.broadcast_to(cells[None], (TAIL, 2 * width)).astype(jnp.bfloat16)
     sent = jnp.concatenate([filtered, cells], axis=0)
-    full = lax.all_gather(sent, AXES, axis=0, tiled=True)
-    devices = full.shape[0] // (own + TAIL)
-    shares = full.reshape(devices, own + TAIL, 2 * width)[:, own, :3]
-    total = jnp.sum(shares.astype(jnp.float32))
-    full = take_rows(full, inverse + inverse // own * TAIL)
+    sends = lax.axis_size("chip") * n_groups
+    block = own + TAIL
+    copies = jnp.broadcast_to(sent[None], (sends, block, 2 * width))
+    mine = lax.all_to_all(copies, ("chip", "modes"), 0, 0)
+    other = lax.ppermute(mine, "core", [(0, 1), (1, 0)])
+    shares = mine[:, own, :3].astype(jnp.float32) + other[:, own, :3].astype(jnp.float32)
+    total = jnp.sum(shares)
+    device = inverse // own
+    pair = device // n_groups
+    side = jnp.where(pair % 2 == core, 0, sends)
+    place = side + pair // 2 * n_groups + device % n_groups
+    tables = [t.reshape(sends * block, 2 * width) for t in (mine, other)]
+    full = take_rows(tables, place * block + inverse % own)
     spectral = synthesize(et, xf, full)
     linear = jnp.dot(features, lin_weight, preferred_element_type=jnp.float32)
     pre = spectral / total + linear + bias[None, :]

time: 252 us -> 236 us (0.937)
  between operations: 18.5 us -> 4.88 us
  waiting for transfers between devices: 108 us -> 100 us
  starting transfers between devices: 7.53 us -> 14.7 us
  matrix products: 5.32 us -> 1.68 us
    all_gather x1 -> x0, waiting for transfers between devices: 61.3 us -> none  [on_device(): full = lax.all_gather(sent, AXES, axis=0, tiled=True)]
    all_to_all x0 -> x1, waiting for transfers between devices: none -> 51.1 us  [on_device(): mine = lax.all_to_all(copies, ('chip', 'modes'), 0, 0)]
    all_to_all x0 -> x1, starting transfers between devices: none -> 4.7 us  [on_device(): mine = lax.all_to_all(copies, ('chip', 'modes'), 0, 0)]
    convert_element_type x0 -> x1, other arithmetic: none -> 3.72 us  [on_device(): return jax.nn.gelu(pre, approximate=False).astype(jnp.bfloat16)]
    dot_general x1, matrix products: 3.91 us -> 0.28 us  [on_device(): linear = jnp.dot(features, lin_weight, preferred_element_type=jnp.float32)]
    ppermute x0 -> x1, starting transfers between devices: none -> 2.65 us  [on_device(): other = lax.ppermute(mine, 'core', [(0, 1), (1, 0)])]
    unnamed x16 -> x14, local copies, waits for them, and re-layouts: 6.92 us -> 5.91 us
  transfers between devices with their start and end apart: 3 -> 4, of which waited for: 3 -> 4; matrix products, arithmetic and copies ran while one was open for 1% -> 1% of each run, Pallas kernels for 0% -> 0%
where the time goes in v4:
time: 236 us; the launch traced here: 235 us
  waiting for transfers between devices  100 us (42%)
  Pallas kernels  88.1 us (37%)
  starting transfers between devices  14.7 us (6%)
  other arithmetic  14.6 us (6%)
  local copies, waits for them, and re-layouts  11 us (5%)
  between operations  4.88 us (2%)
    all_to_all x1, waiting for transfers between devices, on_device(): mine = lax.all_to_all(copies, ('chip', 'modes'), 0, 0)  51.1 us
    pallas_call x2, Pallas kernels, take_rows(): pl.pallas_call(take_kernel, out_shape=jax.ShapeDtypeStruct((m, width), ta...  43.8 us
    all_to_all x1, waiting for transfers between devices, on_device(): lax.all_to_all(both.reshape(-1, own, 2 * width), ('chip', 'modes'), 0, 0)  43.4 us
    pallas_call x1, Pallas kernels, filter_modes(): pl.pallas_call(filter_kernel, grid=(modes // step,), out_shape=jax.ShapeD...  13.9 us
    pallas_call x1, Pallas kernels, analyse(): pl.pallas_call(analyse_kernel, grid=(HALF,), out_shape=jax.ShapeDtypeStru...  13.5 us
    pallas_call x1, Pallas kernels, synthesize(): pl.pallas_call(synthesize_kernel, grid=(HALF,), out_shape=jax.ShapeDtypeS...  13.4 us
    all_to_all x1, starting transfers between devices, on_device(): lax.all_to_all(both.reshape(-1, own, 2 * width), ('chip', 'modes'), 0, 0)  6.64 us
    unnamed x14, local copies, waits for them, and re-layouts  5.91 us
  transfers between devices with their start and end apart: 4, of which 4 were waited for; matrix products, arithmetic and copies ran while one was open for 1% of the time, Pallas kernels for 0%

profile of v4, /device:TPU:11, one launch (start us, length us, event | category | flops | bytes accessed | tf_op | source)
XLA Modules:
  0.0 235.2 jit_solution(11236203756955117442)
XLA Ops:
  0.0 0.0 copy-start
  0.0 0.0 copy-start.4
  0.0 1.0 fusion.66
  1.0 0.3 fusion.30
  1.4 0.3 copy.8
  1.7 1.3 fusion.63
  3.0 1.3 fusion.65
  4.3 1.0 fusion.19
  5.3 0.5 fusion.22
  5.8 0.0 copy-done.4
  5.8 0.3 multiply_convert_fusion.weighted_ref
  6.2 3.5 %shard_map.73 = (bf16[1024,2048]{1,0:T(8,128)(2,1)S(1)}, bf16[2048,1024]{1,0:T(8,128)(2,1)}) custom-call(f32[16,2048]{1,0:T(8,128)S(1)} %get-tuple-element.30.yc_ref, f32[16,2048]{1,0:T(8,128)S(1)} %get-tuple-element.29.ys_ref, f32[32,2048]{1,0:T(8,128)S(1)} %get-tuple-element.26.zc_ref, f32[32,2048]{1,0:T(8,128)S(1)} %get-tuple-element.25.zs_ref), custom_call_target="tpu_custom_call" | custom-call | tf_op jit(solution)/shard_map/pallas_call | solution.py:51
  9.7 0.0 copy-start.3
  9.7 2.0 copy-done.3
  11.7 13.5 %shard_map.74 = bf16[2,8,512,256]{3,2,1,0:T(8,128)(2,1)S(1)} custom-call(bf16[1024,2048]{1,0:T(8,128)(2,1)} %copy-done.3, f32[2048,16]{1,0:T(8,128)S(1)} %bitcast.31, bf16[2048,128]{1,0:T(8,128)(2,1)S(1)} %multiply_convert_fusion.weighted_ref), custom_call_target="tpu_custom_call" | custom-call | tf_op jit(solution)/shard_map/pallas_call | solution.py:91
  25.2 0.0 copy-start.2
  25.2 2.0 copy-done.2
  27.2 22.3 %shard_map.75 = bf16[8192,256]{1,0:T(8,128)(2,1)S(1)} custom-call(s32[8192]{0:T(1024)S(1)} %get-tuple-element.12.index_ref, bf16[8192,256]{1,0:T(8,128)(2,1)} %bitcast.30), custom_call_target="tpu_custom_call" | custom-call | tf_op jit(solution)/shard_map/pallas_call | solution.py:200
  49.5 0.0 copy-start.1
  49.5 2.0 copy-done.1
  51.4 3.2 %dynamic-slice_bitcast_fusion = bf16[8,2,256,256]{3,2,1,0:T(8,128)(2,1)} fusion(bf16[8,2,2,256,256]{4,3,2,1,0:T(8,128)(2,1)} %bitcast.28, s32[]{:T(128)S(6)} %select_n.113), kind=kLoop, calls=%fused_computation.7 | loop fusion | bytes 4194308 | tf_op jit(solution)/shard_map/jit(dynamic_index_in_dim)/squeeze | solution.py:254
  54.6 0.7 collective-permute-start
  55.3 4.0 %collective-permute-done = bf16[8,2,256,256]{3,2,1,0:T(8,128)(2,1)S(1)} collective-permute-done((bf16[8,2,256,256]{3,2,1,0:T(8,128)(2,1)}, bf16[8,2,256,256]{3,2,1,0:T(8,128)(2,1)S(1)}, u32[]{:S(2)}, u32[]{:S(2)}) %collective-permute-start) | collective-permute-done | bytes 2097184 | tf_op jit(solution)/shard_map/ppermute | solution.py:256
  59.2 3.6 %fusion = bf16[8,2,256,256]{3,2,1,0:T(8,128)(2,1)} fusion(bf16[8,2,256,256]{3,2,1,0:T(8,128)(2,1)S(1)} %collective-permute-done, bf16[8,2,2,256,256]{4,3,2,1,0:T(8,128)(2,1)} %bitcast.29, s32[]{:T(128)S(6)} %select_n.112), kind=kLoop, calls=%fused_computation.1 | loop fusion | flops 4194304 | bytes 6291460 | tf_op jit(solution)/shard_map/convert_element_type | solution.py:257
  62.8 6.6 %all-to-all-start = ((bf16[16,256,256]{2,1,0:T(8,128)(2,1)}), bf16[16,256,256]{2,1,0:T(8,128)(2,1)S(1)}, u32[]{:S(2)}, u32[]{:S(2)}) async-start(bf16[16,256,256]{2,1,0:T(8,128)(2,1)} %bitcast.14), calls=%async_computation | async-start | bytes 4194304 | tf_op jit(solution)/shard_map/all_to_all | solution.py:258
  74.2 0.1 fusion.61
  74.2 43.4 %all-to-all-done = bf16[16,256,256]{2,1,0:T(8,128)(2,1)S(1)} async-done(((bf16[16,256,256]{2,1,0:T(8,128)(2,1)}), bf16[16,256,256]{2,1,0:T(8,128)(2,1)S(1)}, u32[]{:S(2)}, u32[]{:S(2)}) %all-to-all-start) | async-done | bytes 2097184 | tf_op jit(solution)/shard_map/all_to_all | solution.py:258
  117.6 0.3 reduce_sum.30
  118.0 13.9 %shard_map.76 = f32[256,256]{1,0:T(8,128)S(1)} custom-call(bf16[256,2,128]{2,1,0:T(2,128)(2,1)S(1)} %reshape.158.coef_ref, bf16[256,2,128,128]{3,2,1,0:T(8,128)(2,1)} %w_ref.1), custom_call_target="tpu_custom_call" | custom-call | tf_op jit(solution)/shard_map/pallas_call | solution.py:158
  131.9 1.5 broadcast_in_dim.30
  133.4 4.7 %all-to-all-start.1 = ((bf16[16,272,256]{2,1,0:T(8,128)(2,1)}), bf16[16,272,256]{2,1,0:T(8,128)(2,1)S(1)}, u32[]{:S(2)}, u32[]{:S(2)}) async-start(bf16[16,272,256]{2,1,0:T(8,128)(2,1)} %broadcast_in_dim.30), calls=%async_computation.1 | async-start | bytes 4456448 | tf_op jit(solution)/shard_map/all_to_all | solution.py:271
  138.1 51.1 %all-to-all-done.1 = bf16[16,272,256]{2,1,0:T(8,128)(2,1)S(1)} async-done(((bf16[16,272,256]{2,1,0:T(8,128)(2,1)}), bf16[16,272,256]{2,1,0:T(8,128)(2,1)S(1)}, u32[]{:S(2)}, u32[]{:S(2)}) %all-to-all-start.1) | async-done | bytes 2228256 | tf_op jit(solution)/shard_map/all_to_all | solution.py:271
  189.2 2.7 %collective-permute-start.1 = (bf16[16,272,256]{2,1,0:T(8,128)(2,1)S(1)}, bf16[16,272,256]{2,1,0:T(8,128)(2,1)S(1)}, u32[]{:S(2)}, u32[]{:S(2)}) collective-permute-start(bf16[16,272,256]{2,1,0:T(8,128)(2,1)S(1)} %all-to-all-done.1), channel_id=1, source_target_pairs={{0,2},{2,0},{1,3},{3,1},{4,6},{6,4},{5,7},{7,5},{8,10},{10,8},{9,1... | collective-permute-start | bytes 6684680 | tf_op jit(solution)/shard_map/ppermute | solution.py:272
  191.9 0.4 select_convert_fusion.1
  192.2 0.0 copy-start.5
  192.2 1.4 fusion.1
  193.6 0.1 fusion.39.index_ref
  193.8 0.0 copy-done
  193.8 0.0 copy-done.5
  193.8 0.3 fusion.16
  194.1 1.8 collective-permute-done.1
  195.8 21.5 %shard_map.77 = bf16[8192,256]{1,0:T(8,128)(2,1)} custom-call(s32[8192]{0:T(1024)S(1)} %fusion.39.index_ref, bf16[4352,256]{1,0:T(8,128)(2,1)S(1)} %bitcast.33, bf16[4352,256]{1,0:T(8,128)(2,1)S(1)} %bitcast.34), custom_call_target="tpu_custom_call" | custom-call | tf_op jit(solution)/shard_map/pallas_call | solution.py:200
  217.4 0.0 copy-start.6
  217.4 13.4 %shard_map.78 = f32[2048,128]{1,0:T(8,128)S(1)} custom-call(bf16[2048,1024]{1,0:T(8,128)(2,1)} %get-tuple-element.7.et_ref, f32[2048,16]{1,0:T(8,128)S(1)} %bitcast.32, bf16[2,8,512,256]{3,2,1,0:T(8,128)(2,1)} %bitcast.35), custom_call_target="tpu_custom_call" | custom-call | tf_op jit(solution)/shard_map/pallas_call | solution.py:131
  230.8 0.7 fusion.55
  231.5 0.0 copy-done.6
  231.5 3.7 %fusion.8 = bf16[2048,128]{1,0:T(8,128)(2,1)} fusion(f32[2048,128]{1,0:T(8,128)S(1)} %fusion.16, f32[2048,128]{1,0:T(8,128)S(1)} %shard_map.78, f32[128]{0:T(128)S(1)} %copy-done.6, f32[]{:T(128)} %fusion.55), kind=kLoop, calls=%fused_computation.15 | loop fusion | flops 17825792 | bytes 2621956 | tf_op jit(solution)/shard_map/convert_element_type | solution.py:284
  (9 shorter events, 0.1 us)
Async XLA Ops:
  0.0 193.8 %copy-start = (bf16[128,128]{1,0:T(8,128)(2,1)S(1)}, bf16[128,128]{1,0:T(8,128)(2,1)}, u32[]{:S(2)}) copy-start(bf16[128,128]{1,0:T(8,128)(2,1)} %param.12) | copy-start | bytes 98308
  0.0 5.8 %copy-start.4 = (bf16[4096,128]{1,0:T(8,128)(2,1)S(1)}, bf16[4096,128]{1,0:T(8,128)(2,1)}, u32[]{:S(2)}) copy-start(bf16[4096,128]{1,0:T(8,128)(2,1)} %param.7) | copy-start | bytes 3145732
  9.7 2.0 copy-start.3
  25.2 2.0 copy-start.2
  49.5 2.0 copy-start.1
  54.6 4.7 %collective-permute-start = (bf16[8,2,256,256]{3,2,1,0:T(8,128)(2,1)}, bf16[8,2,256,256]{3,2,1,0:T(8,128)(2,1)S(1)}, u32[]{:S(2)}, u32[]{:S(2)}) collective-permute-start(bf16[8,2,256,256]{3,2,1,0:T(8,128)(2,1)} %dynamic-slice_bitcast_fusion), channel_id=1, source_target_pairs={{0,2},{2,0},{1,3},{3,1},{4,6},{6,4},{5,7},{7,5},{8,10},{10,8},{9,1... | collective-permute-start | bytes 6291464 | tf_op jit(solution)/shard_map/ppermute | solution.py:256
  62.8 54.8 %all-to-all-start = ((bf16[16,256,256]{2,1,0:T(8,128)(2,1)}), bf16[16,256,256]{2,1,0:T(8,128)(2,1)S(1)}, u32[]{:S(2)}, u32[]{:S(2)}) async-start(bf16[16,256,256]{2,1,0:T(8,128)(2,1)} %bitcast.14), calls=%async_computation | async-start | bytes 4194304 | tf_op jit(solution)/shard_map/all_to_all | solution.py:258
  133.4 55.8 %all-to-all-start.1 = ((bf16[16,272,256]{2,1,0:T(8,128)(2,1)}), bf16[16,272,256]{2,1,0:T(8,128)(2,1)S(1)}, u32[]{:S(2)}, u32[]{:S(2)}) async-start(bf16[16,272,256]{2,1,0:T(8,128)(2,1)} %broadcast_in_dim.30), calls=%async_computation.1 | async-start | bytes 4456448 | tf_op jit(solution)/shard_map/all_to_all | solution.py:271
  189.2 6.6 %collective-permute-start.1 = (bf16[16,272,256]{2,1,0:T(8,128)(2,1)S(1)}, bf16[16,272,256]{2,1,0:T(8,128)(2,1)S(1)}, u32[]{:S(2)}, u32[]{:S(2)}) collective-permute-start(bf16[16,272,256]{2,1,0:T(8,128)(2,1)S(1)} %all-to-all-done.1), channel_id=1, source_target_pairs={{0,2},{2,0},{1,3},{3,1},{4,6},{6,4},{5,7},{7,5},{8,10},{10,8},{9,1... | collective-permute-start | bytes 6684680 | tf_op jit(solution)/shard_map/ppermute | solution.py:272
  192.2 1.5 copy-start.5
  217.4 14.1 %copy-start.6 = (f32[128]{0:T(128)S(1)}, f32[128]{0:T(128)}, u32[]{:S(2)}) copy-start(f32[128]{0:T(128)} %param.13) | copy-start | bytes 1540

commit v5 on v4

--- a/solution.py
+++ b/solution.py
@@ -154,7 +154,7 @@
 
 def filter_modes(coef, weight):
     modes, width = weight.shape[0], weight.shape[2]
-    step = math.gcd(modes, 16)
+    step = math.gcd(modes, 32)
     return pl.pallas_call(
         filter_kernel,
         grid=(modes // step,),
@@ -179,7 +179,7 @@
 
     rows = out_ref.shape[0]
     base = pl.program_id(0) * rows
-    unroll = math.gcd(rows, 16)
+    unroll = math.gcd(rows, 32)
 
     def body(block, carry):
         at = block * unroll

time: 236 us -> 229 us (0.970)
  Pallas kernels: 88.1 us -> 81.6 us
    pallas_call x1, Pallas kernels: 13.9 us -> 10.1 us  [filter_modes(): pl.pallas_call(filter_kernel, grid=(modes // step,), out_shape=jax.ShapeD...]
    pallas_call x2, Pallas kernels: 43.8 us -> 41 us  [take_rows(): pl.pallas_call(take_kernel, out_shape=jax.ShapeDtypeStruct((m, width), ta...]
where the time goes in v5:
time: 229 us
  waiting for transfers between devices  100 us (44%)
  Pallas kernels  81.6 us (36%)
  starting transfers between devices  14.7 us (6%)
  other arithmetic  14.6 us (6%)
  local copies, waits for them, and re-layouts  11 us (5%)
  between operations  4.88 us (2%)
    all_to_all x1, waiting for transfers between devices, on_device(): mine = lax.all_to_all(copies, ('chip', 'modes'), 0, 0)  51.1 us
    all_to_all x1, waiting for transfers between devices, on_device(): lax.all_to_all(both.reshape(-1, own, 2 * width), ('chip', 'modes'), 0, 0)  43.4 us
    pallas_call x2, Pallas kernels, take_rows(): pl.pallas_call(take_kernel, out_shape=jax.ShapeDtypeStruct((m, width), ta...  41 us
    pallas_call x1, Pallas kernels, analyse(): pl.pallas_call(analyse_kernel, grid=(HALF,), out_shape=jax.ShapeDtypeStru...  13.5 us
    pallas_call x1, Pallas kernels, synthesize(): pl.pallas_call(synthesize_kernel, grid=(HALF,), out_shape=jax.ShapeDtypeS...  13.4 us
    pallas_call x1, Pallas kernels, filter_modes(): pl.pallas_call(filter_kernel, grid=(modes // step,), out_shape=jax.ShapeD...  10.1 us
    all_to_all x1, starting transfers between devices, on_device(): lax.all_to_all(both.reshape(-1, own, 2 * width), ('chip', 'modes'), 0, 0)  6.64 us
    unnamed x14, local copies, waits for them, and re-layouts  5.91 us
  transfers between devices with their start and end apart: 4, of which 4 were waited for; matrix products, arithmetic and copies ran while one was open for 1% of the time, Pallas kernels for 0%

profile of v5, /device:TPU:11, one launch (start us, length us, event | category | flops | bytes accessed | tf_op | source)
XLA Modules:
  0.0 228.6 jit_solution(1790860720811149429)
XLA Ops:
  0.0 0.0 copy-start
  0.0 0.0 copy-start.4
  0.0 1.0 fusion.66
  1.0 0.3 fusion.30
  1.4 0.3 copy.8
  1.7 1.3 fusion.63
  3.0 1.3 fusion.65
  4.3 1.0 fusion.19
  5.3 0.5 fusion.22
  5.8 0.0 copy-done.4
  5.8 0.3 multiply_convert_fusion.weighted_ref
  6.2 3.5 %shard_map.73 = (bf16[1024,2048]{1,0:T(8,128)(2,1)S(1)}, bf16[2048,1024]{1,0:T(8,128)(2,1)}) custom-call(f32[16,2048]{1,0:T(8,128)S(1)} %get-tuple-element.30.yc_ref, f32[16,2048]{1,0:T(8,128)S(1)} %get-tuple-element.29.ys_ref, f32[32,2048]{1,0:T(8,128)S(1)} %get-tuple-element.26.zc_ref, f32[32,2048]{1,0:T(8,128)S(1)} %get-tuple-element.25.zs_ref), custom_call_target="tpu_custom_call" | custom-call | tf_op jit(solution)/shard_map/pallas_call | solution.py:51
  9.7 0.0 copy-start.3
  9.7 2.0 copy-done.3
  11.7 13.5 %shard_map.74 = bf16[2,8,512,256]{3,2,1,0:T(8,128)(2,1)S(1)} custom-call(bf16[1024,2048]{1,0:T(8,128)(2,1)} %copy-done.3, f32[2048,16]{1,0:T(8,128)S(1)} %bitcast.31, bf16[2048,128]{1,0:T(8,128)(2,1)S(1)} %multiply_convert_fusion.weighted_ref), custom_call_target="tpu_custom_call" | custom-call | tf_op jit(solution)/shard_map/pallas_call | solution.py:91
  25.2 0.0 copy-start.2
  25.2 2.0 copy-done.2
  27.2 21.0 %shard_map.75 = bf16[8192,256]{1,0:T(8,128)(2,1)S(1)} custom-call(s32[8192]{0:T(1024)S(1)} %get-tuple-element.12.index_ref, bf16[8192,256]{1,0:T(8,128)(2,1)} %bitcast.30), custom_call_target="tpu_custom_call" | custom-call | tf_op jit(solution)/shard_map/pallas_call | solution.py:200
  48.2 0.0 copy-start.1
  48.2 2.0 copy-done.1
  50.2 3.2 %dynamic-slice_bitcast_fusion = bf16[8,2,256,256]{3,2,1,0:T(8,128)(2,1)} fusion(bf16[8,2,2,256,256]{4,3,2,1,0:T(8,128)(2,1)} %bitcast.28, s32[]{:T(128)S(6)} %select_n.113), kind=kLoop, calls=%fused_computation.7 | loop fusion | bytes 4194308 | tf_op jit(solution)/shard_map/jit(dynamic_index_in_dim)/squeeze | solution.py:254
  53.4 0.7 collective-permute-start
  54.0 4.0 %collective-permute-done = bf16[8,2,256,256]{3,2,1,0:T(8,128)(2,1)S(1)} collective-permute-done((bf16[8,2,256,256]{3,2,1,0:T(8,128)(2,1)}, bf16[8,2,256,256]{3,2,1,0:T(8,128)(2,1)S(1)}, u32[]{:S(2)}, u32[]{:S(2)}) %collective-permute-start) | collective-permute-done | bytes 2097184 | tf_op jit(solution)/shard_map/ppermute | solution.py:256
  58.0 3.6 %fusion = bf16[8,2,256,256]{3,2,1,0:T(8,128)(2,1)} fusion(bf16[8,2,256,256]{3,2,1,0:T(8,128)(2,1)S(1)} %collective-permute-done, bf16[8,2,2,256,256]{4,3,2,1,0:T(8,128)(2,1)} %bitcast.29, s32[]{:T(128)S(6)} %select_n.112), kind=kLoop, calls=%fused_computation.1 | loop fusion | flops 4194304 | bytes 6291460 | tf_op jit(solution)/shard_map/convert_element_type | solution.py:257
  61.6 6.6 %all-to-all-start = ((bf16[16,256,256]{2,1,0:T(8,128)(2,1)}), bf16[16,256,256]{2,1,0:T(8,128)(2,1)S(1)}, u32[]{:S(2)}, u32[]{:S(2)}) async-start(bf16[16,256,256]{2,1,0:T(8,128)(2,1)} %bitcast.14), calls=%async_computation | async-start | bytes 4194304 | tf_op jit(solution)/shard_map/all_to_all | solution.py:258
  73.0 0.1 fusion.61
  73.0 43.4 %all-to-all-done = bf16[16,256,256]{2,1,0:T(8,128)(2,1)S(1)} async-done(((bf16[16,256,256]{2,1,0:T(8,128)(2,1)}), bf16[16,256,256]{2,1,0:T(8,128)(2,1)S(1)}, u32[]{:S(2)}, u32[]{:S(2)}) %all-to-all-start) | async-done | bytes 2097184 | tf_op jit(solution)/shard_map/all_to_all | solution.py:258
  116.4 0.3 reduce_sum.30
  116.7 10.1 %shard_map.76 = f32[256,256]{1,0:T(8,128)S(1)} custom-call(bf16[256,2,128]{2,1,0:T(2,128)(2,1)S(1)} %reshape.158.coef_ref, bf16[256,2,128,128]{3,2,1,0:T(8,128)(2,1)} %w_ref.1), custom_call_target="tpu_custom_call" | custom-call | tf_op jit(solution)/shard_map/pallas_call | solution.py:158
  126.9 1.5 broadcast_in_dim.30
  128.5 4.7 %all-to-all-start.1 = ((bf16[16,272,256]{2,1,0:T(8,128)(2,1)}), bf16[16,272,256]{2,1,0:T(8,128)(2,1)S(1)}, u32[]{:S(2)}, u32[]{:S(2)}) async-start(bf16[16,272,256]{2,1,0:T(8,128)(2,1)} %broadcast_in_dim.30), calls=%async_computation.1 | async-start | bytes 4456448 | tf_op jit(solution)/shard_map/all_to_all | solution.py:271
  133.2 51.1 %all-to-all-done.1 = bf16[16,272,256]{2,1,0:T(8,128)(2,1)S(1)} async-done(((bf16[16,272,256]{2,1,0:T(8,128)(2,1)}), bf16[16,272,256]{2,1,0:T(8,128)(2,1)S(1)}, u32[]{:S(2)}, u32[]{:S(2)}) %all-to-all-start.1) | async-done | bytes 2228256 | tf_op jit(solution)/shard_map/all_to_all | solution.py:271
  184.3 2.7 %collective-permute-start.1 = (bf16[16,272,256]{2,1,0:T(8,128)(2,1)S(1)}, bf16[16,272,256]{2,1,0:T(8,128)(2,1)S(1)}, u32[]{:S(2)}, u32[]{:S(2)}) collective-permute-start(bf16[16,272,256]{2,1,0:T(8,128)(2,1)S(1)} %all-to-all-done.1), channel_id=1, source_target_pairs={{0,2},{2,0},{1,3},{3,1},{4,6},{6,4},{5,7},{7,5},{8,10},{10,8},{9,1... | collective-permute-start | bytes 6684680 | tf_op jit(solution)/shard_map/ppermute | solution.py:272
  186.9 0.4 select_convert_fusion.1
  187.3 0.0 copy-start.5
  187.3 1.4 fusion.1
  188.7 0.1 fusion.39.index_ref
  188.8 0.0 copy-done
  188.8 0.0 copy-done.5
  188.8 0.3 fusion.16
  189.1 1.8 collective-permute-done.1
  190.9 19.9 %shard_map.77 = bf16[8192,256]{1,0:T(8,128)(2,1)} custom-call(s32[8192]{0:T(1024)S(1)} %fusion.39.index_ref, bf16[4352,256]{1,0:T(8,128)(2,1)S(1)} %bitcast.33, bf16[4352,256]{1,0:T(8,128)(2,1)S(1)} %bitcast.34), custom_call_target="tpu_custom_call" | custom-call | tf_op jit(solution)/shard_map/pallas_call | solution.py:200
  210.8 0.0 copy-start.6
  210.8 13.4 %shard_map.78 = f32[2048,128]{1,0:T(8,128)S(1)} custom-call(bf16[2048,1024]{1,0:T(8,128)(2,1)} %get-tuple-element.7.et_ref, f32[2048,16]{1,0:T(8,128)S(1)} %bitcast.32, bf16[2,8,512,256]{3,2,1,0:T(8,128)(2,1)} %bitcast.35), custom_call_target="tpu_custom_call" | custom-call | tf_op jit(solution)/shard_map/pallas_call | solution.py:131
  224.3 0.7 fusion.55
  224.9 0.0 copy-done.6
  224.9 3.7 %fusion.8 = bf16[2048,128]{1,0:T(8,128)(2,1)} fusion(f32[2048,128]{1,0:T(8,128)S(1)} %fusion.16, f32[2048,128]{1,0:T(8,128)S(1)} %shard_map.78, f32[128]{0:T(128)S(1)} %copy-done.6, f32[]{:T(128)} %fusion.55), kind=kLoop, calls=%fused_computation.15 | loop fusion | flops 17825792 | bytes 2621956 | tf_op jit(solution)/shard_map/convert_element_type | solution.py:284
  (9 shorter events, 0.1 us)
Async XLA Ops:
  0.0 188.8 %copy-start = (bf16[128,128]{1,0:T(8,128)(2,1)S(1)}, bf16[128,128]{1,0:T(8,128)(2,1)}, u32[]{:S(2)}) copy-start(bf16[128,128]{1,0:T(8,128)(2,1)} %param.12) | copy-start | bytes 98308
  0.0 5.8 %copy-start.4 = (bf16[4096,128]{1,0:T(8,128)(2,1)S(1)}, bf16[4096,128]{1,0:T(8,128)(2,1)}, u32[]{:S(2)}) copy-start(bf16[4096,128]{1,0:T(8,128)(2,1)} %param.7) | copy-start | bytes 3145732
  9.7 2.0 copy-start.3
  25.2 2.0 copy-start.2
  48.2 2.0 copy-start.1
  53.4 4.7 %collective-permute-start = (bf16[8,2,256,256]{3,2,1,0:T(8,128)(2,1)}, bf16[8,2,256,256]{3,2,1,0:T(8,128)(2,1)S(1)}, u32[]{:S(2)}, u32[]{:S(2)}) collective-permute-start(bf16[8,2,256,256]{3,2,1,0:T(8,128)(2,1)} %dynamic-slice_bitcast_fusion), channel_id=1, source_target_pairs={{0,2},{2,0},{1,3},{3,1},{4,6},{6,4},{5,7},{7,5},{8,10},{10,8},{9,1... | collective-permute-start | bytes 6291464 | tf_op jit(solution)/shard_map/ppermute | solution.py:256
  61.6 54.8 %all-to-all-start = ((bf16[16,256,256]{2,1,0:T(8,128)(2,1)}), bf16[16,256,256]{2,1,0:T(8,128)(2,1)S(1)}, u32[]{:S(2)}, u32[]{:S(2)}) async-start(bf16[16,256,256]{2,1,0:T(8,128)(2,1)} %bitcast.14), calls=%async_computation | async-start | bytes 4194304 | tf_op jit(solution)/shard_map/all_to_all | solution.py:258
  128.5 55.8 %all-to-all-start.1 = ((bf16[16,272,256]{2,1,0:T(8,128)(2,1)}), bf16[16,272,256]{2,1,0:T(8,128)(2,1)S(1)}, u32[]{:S(2)}, u32[]{:S(2)}) async-start(bf16[16,272,256]{2,1,0:T(8,128)(2,1)} %broadcast_in_dim.30), calls=%async_computation.1 | async-start | bytes 4456448 | tf_op jit(solution)/shard_map/all_to_all | solution.py:271
  184.3 6.6 %collective-permute-start.1 = (bf16[16,272,256]{2,1,0:T(8,128)(2,1)S(1)}, bf16[16,272,256]{2,1,0:T(8,128)(2,1)S(1)}, u32[]{:S(2)}, u32[]{:S(2)}) collective-permute-start(bf16[16,272,256]{2,1,0:T(8,128)(2,1)S(1)} %all-to-all-done.1), channel_id=1, source_target_pairs={{0,2},{2,0},{1,3},{3,1},{4,6},{6,4},{5,7},{7,5},{8,10},{10,8},{9,1... | collective-permute-start | bytes 6684680 | tf_op jit(solution)/shard_map/ppermute | solution.py:272
  187.3 1.5 copy-start.5
  210.8 14.1 %copy-start.6 = (f32[128]{0:T(128)S(1)}, f32[128]{0:T(128)}, u32[]{:S(2)}) copy-start(f32[128]{0:T(128)} %param.13) | copy-start | bytes 1540
